TPU v7x, 32 devices: a whole 2x2x4 slice. The times are simulated.
32 devices in a mesh: rows: 16 (over z, x, core), cols: 2 (over y).
Axes of the slice: x: 2, y: 2, z: 4, core: 2. Of those that a mesh axis runs over, the one named last changes fastest.
Arguments:
- cells: bfloat16 [2048, 768], P('rows', 'cols'), may hold values from -6 to 6
- feat_mask: int32 [2048, 4], P('rows'), may hold values from 0 to 1, as said below
- train_rows: int32 [1], replicated, may hold values from 512 to 1536
- cotangent: bfloat16 [2048, 768], P('rows', 'cols'), may hold values from -6 to 6
- proj_weights: float32 [6, 192, 192], replicated, may hold values from -0.625 to 0.625
- feat_out_w: float32 [192, 192], replicated, may hold values from -0.75 to 0.75
- item_out_w: float32 [192, 192], replicated, may hold values from -2 to 2
- mlp_in: float32 [192, 384], replicated, may hold values from -0.4375 to 0.4375
- mlp_out: float32 [384, 192], replicated, may hold values from -0.3125 to 0.3125
- norm_gains: float32 [3, 192], replicated, may hold values from 0.5 to 1.5
- norm_shifts: float32 [3, 192], replicated, may hold values from -1.8 to 1.8
- bases_small: float32 [18, 192, 192], replicated, may hold values from -1 to 1, as said below
- bases_big: float32 [2, 384, 384], replicated, may hold values from -1 to 1, as said below
- owner_rows: int32 [2304], replicated, may hold values from 0 to 2303, each once
- bank_first: float32 [2304, 192], P('rows'), may hold values from -0.0010000406 to 0.0010000406
- bank_second: float32 [2304, 192], P('rows'), may hold values from 1.1859668e-07 to 4.746122e-07
- norm_first: float32 [2, 3, 192], replicated, may hold values from -0.0010000406 to 0.0010000406
- norm_second: float32 [2, 3, 192], replicated, may hold values from 1.1859668e-07 to 4.746122e-07
Outputs:
- layer_out: bfloat16 [2048, 768], P('rows', 'cols')
- cells_grad: float32 [2048, 768], P('rows', 'cols')
- square_grads: float32 [8, 192, 192], replicated
- mlp_in_grad: float32 [192, 384], replicated
- mlp_out_grad: float32 [384, 192], replicated
- norm_grads: float32 [2, 3, 192], replicated
- clip_norm: float32 [1], replicated
- bank_first_new: float32 [2304, 192], P('rows')
- bank_second_new: float32 [2304, 192], P('rows')
- square_new: float32 [8, 192, 192], replicated
- mlp_in_new: float32 [192, 384], replicated
- mlp_out_new: float32 [384, 192], replicated
- square_low: bfloat16 [8, 192, 192], replicated
- mlp_in_low: bfloat16 [192, 384], replicated
- mlp_out_low: bfloat16 [384, 192], replicated
- norm_new: float32 [2, 3, 192], replicated
- norm_first_new: float32 [2, 3, 192], replicated
- norm_second_new: float32 [2, 3, 192], replicated
Inputs may be any that keep to these rules, and one draw needn't show every extreme that they name: `feat_mask`: every row has at least one 1. rows 0 to train_rows - 1 are the training rows. `owner_rows`: each number once. `bases_small`: each matrix is orthogonal. `bases_big`: each matrix is orthogonal.
All inputs are finite; a program needn't handle non-finite values.
Results may differ from a plain program's by a relative error of at most 0.02.
The roundings to bfloat16 on the way count: a program that leaves them out, or rounds other values in their place, can miss the bound.
Values may be sent and summed in bfloat16 or wider, within the bound.
A program may use at most 192 MiB of HBM per device.

v0:
```python
import functools
import math

import jax
import jax.numpy as jnp
from jax import lax
from jax.experimental import pallas as pl
from jax.experimental.pallas import tpu as pltpu
from jax.sharding import PartitionSpec as P

HEADS = 6
STEP = 10


HIGHEST = lax.Precision.HIGHEST
NEGATIVE = -1e30
CLIP_NORM = 1.0
BETA_ONE = 0.9
BETA_TWO = 0.95
EPSILON = 1e-08
LEARN_RATE = 1.0


def layer_norm(hidden, gain_row, shift_row):
    center = jnp.mean(hidden, axis=-1, keepdims=True)
    centered = hidden - center
    spread = jnp.mean(centered * centered, axis=-1, keepdims=True)
    return centered * lax.rsqrt(spread + 1e-05) * gain_row + shift_row


def gelu_exact(hidden):
    return jax.nn.gelu(hidden, approximate=False)


def product(left_side, right_side):
    return jnp.dot(left_side, right_side, preferred_element_type=jnp.float32)


def product_left(left_side, right_side):
    return lax.dot_general(
        left_side, right_side, (((0,), (0,)), ((), ())), preferred_element_type=jnp.float32
    )


def product_right(left_side, right_side):
    return lax.dot_general(
        left_side, right_side, (((1,), (1,)), ((), ())), preferred_element_type=jnp.float32
    )


def feature_forward(queries, key_rows, value_rows, key_open):
    scaling = queries.shape[-1] ** (-0.5)
    scores = (
        jnp.einsum("nqhe,nkhe->nhqk", queries, key_rows, preferred_element_type=jnp.float32)
        * scaling
    )
    scores = jnp.where(key_open[:, None, None, :], scores, NEGATIVE)
    attend = jax.nn.softmax(scores, axis=-1)
    attend_low = attend.astype(jnp.bfloat16)
    mixed = jnp.einsum(
        "nhqk,nkhe->nqhe", attend_low, value_rows, preferred_element_type=jnp.float32
    )
    return (attend, attend_low, mixed.astype(jnp.bfloat16))


def feature_backward(queries, key_rows, value_rows, attend, attend_low, mixed_grad):
    scaling = queries.shape[-1] ** (-0.5)
    value_dots = jnp.einsum(
        "nqhe,nkhe->nhqk", mixed_grad, value_rows, preferred_element_type=jnp.float32
    )
    row_delta = jnp.sum(attend * value_dots, axis=-1, keepdims=True)
    score_grad = (attend * (value_dots - row_delta)).astype(jnp.bfloat16)
    query_grad = (
        jnp.einsum("nhqk,nkhe->nqhe", score_grad, key_rows, preferred_element_type=jnp.float32)
        * scaling
    )
    key_grad = (
        jnp.einsum("nhqk,nqhe->nkhe", score_grad, queries, preferred_element_type=jnp.float32)
        * scaling
    )
    value_grad = jnp.einsum(
        "nhqk,nqhe->nkhe", attend_low, mixed_grad, preferred_element_type=jnp.float32
    )
    return (
        query_grad.astype(jnp.bfloat16),
        key_grad.astype(jnp.bfloat16),
        value_grad.astype(jnp.bfloat16),
    )


def key_blocks_of(key_rows, value_rows):
    key_total = key_rows.shape[0]
    block_size = math.gcd(key_total, 1024)
    block_count = key_total // block_size
    tail_shape = key_rows.shape[1:]
    starts = jnp.arange(block_count, dtype=jnp.int32) * block_size
    return (
        key_rows.reshape((block_count, block_size) + tail_shape),
        value_rows.reshape((block_count, block_size) + tail_shape),
        starts,
    )


def block_scores(queries, key_block, start_row, train_count):
    scaling = queries.shape[-1] ** (-0.5)
    scores = (
        jnp.einsum("qche,kche->chqk", queries, key_block, preferred_element_type=jnp.float32)
        * scaling
    )
    open_keys = start_row + jnp.arange(key_block.shape[0], dtype=jnp.int32) < train_count
    return jnp.where(open_keys[None, None, None, :], scores, NEGATIVE)


def item_forward(queries, key_rows, value_rows, train_count):
    key_split, value_split, starts = key_blocks_of(key_rows, value_rows)
    stat_shape = (queries.shape[1], queries.shape[2], queries.shape[0])

    def max_pass(carried, packed):
        running_max, running_sum = carried
        key_block, start_row = packed
        scores = block_scores(queries, key_block, start_row, train_count)
        new_max = jnp.maximum(running_max, jnp.max(scores, axis=-1))
        running_sum = running_sum * jnp.exp(running_max - new_max) + jnp.sum(
            jnp.exp(scores - new_max[..., None]), axis=-1
        )
        return ((new_max, running_sum), None)

    start_max = jnp.full(stat_shape, NEGATIVE, jnp.float32)
    (row_max, row_sum), _ = lax.scan(
        max_pass, (start_max, jnp.zeros(stat_shape, jnp.float32)), (key_split, starts)
    )
    log_total = row_max + jnp.log(row_sum)

    def value_pass(carried, packed):
        key_block, value_block, start_row = packed
        attend = jnp.exp(
            block_scores(queries, key_block, start_row, train_count) - log_total[..., None]
        )
        added = jnp.einsum(
            "chqk,kche->qche",
            attend.astype(jnp.bfloat16),
            value_block,
            preferred_element_type=jnp.float32,
        )
        return (carried + added, None)

    item_full, _ = lax.scan(
        value_pass, jnp.zeros(queries.shape, jnp.float32), (key_split, value_split, starts)
    )
    return (log_total, item_full)


def delta_of(mixed_grad, item_full):
    return jnp.transpose(jnp.sum(mixed_grad.astype(jnp.float32) * item_full, axis=-1), (1, 2, 0))


def item_backward(queries, key_rows, value_rows, train_count, log_total, mixed_grad, item_full):
    key_split, value_split, starts = key_blocks_of(key_rows, value_rows)
    scaling = queries.shape[-1] ** (-0.5)
    row_delta = delta_of(mixed_grad, item_full)

    def back_pass(carried, packed):
        key_block, value_block, start_row = packed
        attend = jnp.exp(
            block_scores(queries, key_block, start_row, train_count) - log_total[..., None]
        )
        value_dots = jnp.einsum(
            "qche,kche->chqk", mixed_grad, value_block, preferred_element_type=jnp.float32
        )
        score_grad = (attend * (value_dots - row_delta[..., None])).astype(jnp.bfloat16)
        carried = carried + jnp.einsum(
            "chqk,kche->qche", score_grad, key_block, preferred_element_type=jnp.float32
        )
        key_grad = (
            jnp.einsum("chqk,qche->kche", score_grad, queries, preferred_element_type=jnp.float32)
            * scaling
        )
        value_grad = jnp.einsum(
            "chqk,qche->kche",
            attend.astype(jnp.bfloat16),
            mixed_grad,
            preferred_element_type=jnp.float32,
        )
        return (carried, (key_grad, value_grad))

    query_sum, (key_grads, value_grads) = lax.scan(
        back_pass, jnp.zeros(queries.shape, jnp.float32), (key_split, value_split, starts)
    )
    key_total = key_rows.shape[0]
    flat_width = queries.shape[1] * queries.shape[2] * queries.shape[3]
    return (
        query_sum * scaling,
        key_grads.reshape(key_total, flat_width),
        value_grads.reshape(key_total, flat_width),
    )


def clip_all(gradients):
    total_sq = jnp.sum(gradients[0] * gradients[0])
    for extra in gradients[1:]:
        total_sq = total_sq + jnp.sum(extra * extra)
    grad_norm = jnp.sqrt(total_sq)
    factor = jnp.minimum(1.0, CLIP_NORM / grad_norm)
    return ([gradient * factor for gradient in gradients], grad_norm)


def rotate_bank(square_grad, in_grad, out_grad, bases_small, bases_big):
    model_width = in_grad.shape[0]
    left_bases = bases_small[0:8]
    right_bases = bases_small[8:16]
    rot_square = jnp.matmul(
        jnp.swapaxes(left_bases, 1, 2),
        jnp.matmul(square_grad, right_bases, precision=HIGHEST),
        precision=HIGHEST,
    )
    rot_in = jnp.dot(
        bases_small[16].T, jnp.dot(in_grad, bases_big[0], precision=HIGHEST), precision=HIGHEST
    )
    rot_out = jnp.dot(
        bases_big[1].T, jnp.dot(out_grad, bases_small[17], precision=HIGHEST), precision=HIGHEST
    )
    return jnp.concatenate(
        [rot_square.reshape(8 * model_width, model_width), rot_in.T, rot_out], axis=0
    )


def rotate_back(step_bank, bases_small, bases_big):
    model_width = step_bank.shape[1]
    ff_width = (step_bank.shape[0] - 8 * model_width) // 2
    step_square = step_bank[: 8 * model_width].reshape(8, model_width, model_width)
    step_in = step_bank[8 * model_width : 8 * model_width + ff_width].T
    step_out = step_bank[8 * model_width + ff_width :]
    up_square = jnp.matmul(
        bases_small[0:8],
        jnp.matmul(step_square, jnp.swapaxes(bases_small[8:16], 1, 2), precision=HIGHEST),
        precision=HIGHEST,
    )
    up_in = jnp.dot(
        bases_small[16], jnp.dot(step_in, bases_big[0].T, precision=HIGHEST), precision=HIGHEST
    )
    up_out = jnp.dot(
        bases_big[1], jnp.dot(step_out, bases_small[17].T, precision=HIGHEST), precision=HIGHEST
    )
    return (up_square, up_in, up_out)


def adam_rows(gradient, first_old, second_old, step_float):
    first_new = BETA_ONE * first_old + (1.0 - BETA_ONE) * gradient
    second_new = BETA_TWO * second_old + (1.0 - BETA_TWO) * gradient * gradient
    first_hat = first_new / (1.0 - jnp.power(BETA_ONE, step_float))
    second_hat = second_new / (1.0 - jnp.power(BETA_TWO, step_float))
    return (first_new, second_new, first_hat / (jnp.sqrt(second_hat) + EPSILON))


def trusted(weight, update, over_axes):
    scaling = jnp.sqrt(jnp.mean(weight * weight, axis=over_axes, keepdims=True) + 1e-06)
    return weight - LEARN_RATE * scaling * update


def per_device(
    cells,
    feat_mask,
    train_rows,
    cotangent,
    proj_weights,
    feat_out_w,
    item_out_w,
    mlp_in,
    mlp_out,
    norm_gains,
    norm_shifts,
    bases_small,
    bases_big,
    owner_rows,
    bank_first,
    bank_second,
    norm_first,
    norm_second,
):
    rows_dev, width_dev = cells.shape
    model_width = proj_weights.shape[-1]
    head_count = HEADS
    head_dim = model_width // head_count
    cols_dev = width_dev // model_width
    col_count = lax.axis_size("cols")
    all_cols = cols_dev * col_count
    half_rows = rows_dev // col_count
    cell_count = rows_dev * cols_dev
    proj_low = proj_weights.astype(jnp.bfloat16)
    feat_qkv = jnp.concatenate([proj_low[0], proj_low[1], proj_low[2]], axis=1)
    item_qkv = jnp.concatenate([proj_low[3], proj_low[4], proj_low[5]], axis=1)
    feat_out_low = feat_out_w.astype(jnp.bfloat16)
    item_out_low = item_out_w.astype(jnp.bfloat16)
    mlp_in_cast = mlp_in.astype(jnp.bfloat16)
    mlp_out_cast = mlp_out.astype(jnp.bfloat16)
    train_count = train_rows[0]
    column_cells = lax.all_to_all(cells, "cols", split_axis=0, concat_axis=1, tiled=True)
    column_flat = column_cells.reshape(half_rows * all_cols, model_width)
    row_mask = (
        lax.dynamic_slice_in_dim(feat_mask, lax.axis_index("cols") * half_rows, half_rows, 0) > 0
    )
    feat_proj = (
        product(column_flat, feat_qkv)
        .astype(jnp.bfloat16)
        .reshape(half_rows, all_cols, 3, head_count, head_dim)
    )
    feat_query = feat_proj[:, :, 0]
    feat_key = feat_proj[:, :, 1]
    feat_value = feat_proj[:, :, 2]
    feat_attend, feat_attend_low, feat_mixed = feature_forward(
        feat_query, feat_key, feat_value, row_mask
    )
    feat_mixed_flat = feat_mixed.reshape(half_rows * all_cols, model_width)
    feat_branch = (
        product(feat_mixed_flat, feat_out_low)
        .astype(jnp.bfloat16)
        .reshape(half_rows, all_cols * model_width)
    )
    feat_back = lax.all_to_all(feat_branch, "cols", split_axis=1, concat_axis=0, tiled=True)
    inputs_flat = cells.astype(jnp.float32).reshape(cell_count, model_width)
    first_sum = inputs_flat + feat_back.astype(jnp.float32).reshape(cell_count, model_width)
    first_out, first_pull = jax.vjp(layer_norm, first_sum, norm_gains[0], norm_shifts[0])
    first_low = first_out.astype(jnp.bfloat16)
    item_proj = product(first_low, item_qkv).astype(jnp.bfloat16)
    item_query = item_proj[:, :model_width].reshape(rows_dev, cols_dev, head_count, head_dim)
    item_key = item_proj[:, model_width : 2 * model_width].reshape(rows_dev, width_dev)
    item_value = item_proj[:, 2 * model_width :].reshape(rows_dev, width_dev)
    key_rows, value_rows = (
        lax.all_gather(item_key, "rows", axis=0, tiled=True),
        lax.all_gather(item_value, "rows", axis=0, tiled=True),
    )
    key_total = key_rows.shape[0]
    key_rows = key_rows.reshape(key_total, cols_dev, head_count, head_dim)
    value_rows = value_rows.reshape(key_total, cols_dev, head_count, head_dim)
    log_total, item_full = item_forward(item_query, key_rows, value_rows, train_count)
    item_low = item_full.astype(jnp.bfloat16).reshape(cell_count, model_width)
    item_branch = product(item_low, item_out_low)
    second_sum = first_out + item_branch
    second_out, second_pull = jax.vjp(layer_norm, second_sum, norm_gains[1], norm_shifts[1])
    second_low = second_out.astype(jnp.bfloat16)
    hidden_pre = product(second_low, mlp_in_cast)
    hidden_act, gelu_pull = jax.vjp(gelu_exact, hidden_pre)
    hidden_low = hidden_act.astype(jnp.bfloat16)
    mlp_branch = product(hidden_low, mlp_out_cast)
    third_sum = second_out + mlp_branch
    third_out, third_pull = jax.vjp(layer_norm, third_sum, norm_gains[2], norm_shifts[2])
    layer_out = third_out.astype(jnp.bfloat16).reshape(rows_dev, width_dev)
    third_grad, gain_three, shift_three = third_pull(
        cotangent.astype(jnp.float32).reshape(cell_count, model_width)
    )
    branch_low = third_grad.astype(jnp.bfloat16)
    mlp_out_grad = product_left(hidden_low, branch_low)
    hidden_grad = product_right(branch_low, mlp_out_cast)
    (pre_grad,) = gelu_pull(hidden_grad)
    pre_low = pre_grad.astype(jnp.bfloat16)
    mlp_in_grad = product_left(second_low, pre_low)
    second_grad = third_grad + product_right(pre_low, mlp_in_cast)
    second_in_grad, gain_two, shift_two = second_pull(second_grad)
    item_branch_low = second_in_grad.astype(jnp.bfloat16)
    item_out_grad = product_left(item_low, item_branch_low)
    item_mixed_grad = (
        product_right(item_branch_low, item_out_low)
        .astype(jnp.bfloat16)
        .reshape(rows_dev, cols_dev, head_count, head_dim)
    )
    key_again, value_again = (
        lax.all_gather(item_key, "rows", axis=0, tiled=True),
        lax.all_gather(item_value, "rows", axis=0, tiled=True),
    )
    key_rows = key_again.reshape(key_total, cols_dev, head_count, head_dim)
    value_rows = value_again.reshape(key_total, cols_dev, head_count, head_dim)
    query_sum, key_grads, value_grads = item_backward(
        item_query, key_rows, value_rows, train_count, log_total, item_mixed_grad, item_full
    )
    key_sum, value_sum = (
        lax.psum_scatter(key_grads, "rows", scatter_dimension=0, tiled=True),
        lax.psum_scatter(value_grads, "rows", scatter_dimension=0, tiled=True),
    )
    item_grad_low = jnp.concatenate(
        [
            query_sum.astype(jnp.bfloat16).reshape(cell_count, model_width),
            key_sum.astype(jnp.bfloat16).reshape(cell_count, model_width),
            value_sum.astype(jnp.bfloat16).reshape(cell_count, model_width),
        ],
        axis=1,
    )
    item_qkv_grad = product_left(first_low, item_grad_low)
    first_grad = second_in_grad + product_right(item_grad_low, item_qkv)
    first_in_grad, gain_one, shift_one = first_pull(first_grad)
    feat_branch_grad = first_in_grad.astype(jnp.bfloat16).reshape(rows_dev, width_dev)
    column_grad = lax.all_to_all(
        feat_branch_grad, "cols", split_axis=0, concat_axis=1, tiled=True
    ).reshape(half_rows * all_cols, model_width)
    feat_out_grad = product_left(feat_mixed_flat, column_grad)
    feat_mixed_grad = (
        product_right(column_grad, feat_out_low)
        .astype(jnp.bfloat16)
        .reshape(half_rows, all_cols, head_count, head_dim)
    )
    feat_query_grad, feat_key_grad, feat_value_grad = feature_backward(
        feat_query, feat_key, feat_value, feat_attend, feat_attend_low, feat_mixed_grad
    )
    feat_grad_low = jnp.concatenate(
        [
            feat_query_grad.reshape(half_rows * all_cols, model_width),
            feat_key_grad.reshape(half_rows * all_cols, model_width),
            feat_value_grad.reshape(half_rows * all_cols, model_width),
        ],
        axis=1,
    )
    feat_qkv_grad = product_left(column_flat, feat_grad_low)
    column_in_grad = (
        product_right(feat_grad_low, feat_qkv)
        .astype(jnp.bfloat16)
        .reshape(half_rows, all_cols * model_width)
    )
    row_in_grad = lax.all_to_all(column_in_grad, "cols", split_axis=1, concat_axis=0, tiled=True)
    cells_grad = first_in_grad.reshape(rows_dev, width_dev) + row_in_grad.astype(jnp.float32)
    proj_grad = jnp.stack(
        [
            feat_qkv_grad[:, :model_width],
            feat_qkv_grad[:, model_width : 2 * model_width],
            feat_qkv_grad[:, 2 * model_width :],
            item_qkv_grad[:, :model_width],
            item_qkv_grad[:, model_width : 2 * model_width],
            item_qkv_grad[:, 2 * model_width :],
        ]
    )
    norm_grad = jnp.stack(
        [
            jnp.stack([gain_one, gain_two, gain_three]),
            jnp.stack([shift_one, shift_two, shift_three]),
        ]
    )
    proj_total, feat_total, item_total, in_total, out_total, norm_total = lax.psum(
        (proj_grad, feat_out_grad, item_out_grad, mlp_in_grad, mlp_out_grad, norm_grad),
        ("rows", "cols"),
    )
    square_grad = jnp.concatenate([proj_total, feat_total[None], item_total[None]], axis=0)
    clipped, grad_norm = clip_all([square_grad, in_total, out_total, norm_total])
    square_clip, in_clip, out_clip, norm_clip = clipped
    rot_bank = rotate_bank(square_clip, in_clip, out_clip, bases_small, bases_big)
    step_float = jnp.asarray(STEP, jnp.float32)
    slot_count = bank_first.shape[0]
    my_slots = lax.dynamic_slice_in_dim(
        owner_rows, lax.axis_index("rows") * slot_count, slot_count, 0
    )
    first_new, second_new, slot_steps = adam_rows(
        jnp.take(rot_bank, my_slots, axis=0), bank_first, bank_second, step_float
    )
    all_steps = lax.all_gather(slot_steps, "rows", axis=0, tiled=True)
    full_steps = jnp.take(all_steps, jnp.argsort(owner_rows), axis=0)
    up_square, up_in, up_out = rotate_back(full_steps, bases_small, bases_big)
    square_old = jnp.concatenate([proj_weights, feat_out_w[None], item_out_w[None]], axis=0)
    square_new = trusted(square_old, up_square, (1, 2))
    in_new = trusted(mlp_in, up_in, (0, 1))
    out_new = trusted(mlp_out, up_out, (0, 1))
    norm_old = jnp.stack([norm_gains, norm_shifts])
    norm_first_new, norm_second_new, norm_steps = adam_rows(
        norm_clip, norm_first, norm_second, step_float
    )
    norm_new = trusted(norm_old, norm_steps, (2,))
    return (
        layer_out,
        cells_grad,
        square_clip,
        in_clip,
        out_clip,
        norm_clip,
        grad_norm.reshape(1),
        first_new,
        second_new,
        square_new,
        in_new,
        out_new,
        square_new.astype(jnp.bfloat16),
        in_new.astype(jnp.bfloat16),
        out_new.astype(jnp.bfloat16),
        norm_new,
        norm_first_new,
        norm_second_new,
    )


F32 = jnp.float32
BF16 = jnp.bfloat16
MESH = pl.DeviceIdType.MESH
VMEM_BYTES = 56 * 1024 * 1024
LANES = 128


def dot_nn(left, right):
    return jnp.dot(left, right, preferred_element_type=F32)


def dot_nt(left, right):
    return lax.dot_general(left, right, (((1,), (1,)), ((), ())), preferred_element_type=F32)


def dot_tn(left, right):
    return lax.dot_general(left, right, (((0,), (0,)), ((), ())), preferred_element_type=F32)


def split_two(value):
    high = value.astype(BF16)
    return high, (value - high.astype(F32)).astype(BF16)


def dot_fine(dot, left, right):
    left_high, left_low = split_two(left)
    right_high, right_low = split_two(right)
    return dot(left_high, right_high) + (dot(left_high, right_low) + dot(left_low, right_high))


def stack_columns(packed, width):
    count = packed.shape[1] // width
    return jnp.concatenate([packed[:, n * width : (n + 1) * width] for n in range(count)], axis=0)


def pack_columns(stacked, rows):
    count = stacked.shape[0] // rows
    return jnp.concatenate([stacked[n * rows : (n + 1) * rows] for n in range(count)], axis=1)


def norm_parts(hidden):
    width = hidden.shape[1]
    center = jnp.sum(hidden, axis=1, keepdims=True) * (1.0 / width)
    centered = hidden - center
    spread = jnp.sum(centered * centered, axis=1, keepdims=True) * (1.0 / width)
    root = lax.rsqrt(spread + 1e-05)
    return centered * root, root


def norm_back(unit, root, gain, incoming):
    width = unit.shape[1]
    scaled = incoming * gain
    mean_one = jnp.sum(scaled, axis=1, keepdims=True) * (1.0 / width)
    mean_two = jnp.sum(scaled * unit, axis=1, keepdims=True) * (1.0 / width)
    gain_grad = jnp.sum(incoming * unit, axis=0, keepdims=True)
    shift_grad = jnp.sum(incoming, axis=0, keepdims=True)
    return root * (scaled - mean_one - unit * mean_two), gain_grad, shift_grad


def head_table(width, head_dim):
    feature = lax.broadcasted_iota(jnp.int32, (width, LANES), 0)
    head = lax.broadcasted_iota(jnp.int32, (width, LANES), 1)
    inside = (feature >= head * head_dim) & (feature < (head + 1) * head_dim)
    return jnp.where(inside, 1.0, 0.0).astype(BF16)


def spread_table(width, head_dim):
    head = lax.broadcasted_iota(jnp.int32, (LANES, width), 0)
    feature = lax.broadcasted_iota(jnp.int32, (LANES, width), 1)
    inside = (feature >= head * head_dim) & (feature < (head + 1) * head_dim)
    return jnp.where(inside, 1.0, 0.0).astype(BF16)


def head_sums(value, table):
    high, low = split_two(value)
    return dot_nn(high, table) + dot_nn(low, table)


def head_mask(rows, width, head_dim, head, offset=0):
    feature = lax.broadcasted_iota(jnp.int32, (rows, width), 1)
    start = offset + head * head_dim
    return (feature >= start) & (feature < start + head_dim)


def tile_rows(value, count):
    return jnp.concatenate([value] * count, axis=0)


def column_open(mask_ref, own_first, cols_dev, slot):
    table = jnp.transpose(mask_ref[...].astype(F32))
    if slot < cols_dev:
        first, second = slot, slot + cols_dev
    else:
        first, second = slot, slot - cols_dev
    picked = jnp.where(own_first, table[:, first : first + 1], table[:, second : second + 1])
    return picked > 0.0


def feature_weights(queries, key_list, open_list, repeat, table, scaling):
    scores = []
    for keys, is_open in zip(key_list, open_list):
        raw = head_sums(queries * tile_rows(keys, repeat), table) * scaling
        scores.append(jnp.where(tile_rows(is_open, repeat), raw, NEGATIVE))
    top = scores[0]
    for extra in scores[1:]:
        top = jnp.maximum(top, extra)
    grown = [jnp.exp(score - top) for score in scores]
    total = grown[0]
    for extra in grown[1:]:
        total = total + extra
    return [part / total for part in grown]


def flip(value, pattern, size):
    out, step = 0, 1
    while step < size:
        out = out + step * (((value // step) % 2 + (pattern // step) % 2) % 2)
        step *= 2
    return out


class RowGather:
    def __init__(self, pieces, send_sem, recv_sem, rows_count):
        self.pieces, self.send_sem, self.recv_sem = pieces, send_sem, recv_sem
        self.deep = rows_count // 4
        me = lax.axis_index("rows")
        self.core, self.side, self.depth = me % 2, (me // 2) % 2, me // 4

    @staticmethod
    def slots(rows_count):
        return rows_count - 1

    def place(self, depth, side, core):
        return (depth * 2 + side) * 2 + core

    def source(self, k):
        return flip(self.depth, k, self.deep)

    def side_peer(self):
        return self.place(self.depth, 1 - self.side, self.core)

    def core_peer(self):
        return self.place(self.depth, self.side, 1 - self.core)

    def copies(self, shard, target, slot):
        return [
            pltpu.make_async_remote_copy(
                src_ref=piece(shard),
                dst_ref=piece(shard),
                send_sem=self.send_sem.at[n, slot],
                recv_sem=self.recv_sem.at[n, slot],
                device_id={"rows": target},
                device_id_type=MESH,
            )
            for n, piece in enumerate(self.pieces)
        ]

    def push(self, shard, target, slot):
        for copy in self.copies(shard, target, slot):
            copy.start()

    def arrive(self, shard, source, slot):
        for copy in self.copies(shard, source, slot):
            copy.wait_recv()

    def start_depth(self):
        own = self.place(self.depth, self.side, self.core)
        for k in range(1, self.deep):
            self.push(own, self.place(self.source(k), self.side, self.core), k - 1)

    def start_near(self):
        own = self.place(self.depth, self.side, self.core)
        self.push(own, self.core_peer(), 2 * self.deep - 1)
        self.push(own, self.side_peer(), self.deep - 1)

    def along_depth(self, k):
        shard = self.place(self.source(k), self.side, self.core)
        self.arrive(shard, shard, k - 1)
        self.push(shard, self.side_peer(), self.deep - 1 + k)
        self.push(shard, self.core_peer(), 2 * self.deep - 1 + k)

    def across_side(self, k):
        shard = self.place(self.source(k), 1 - self.side, self.core)
        self.arrive(shard, self.side_peer(), self.deep - 1 + k)
        self.push(shard, self.core_peer(), 3 * self.deep - 1 + k)

    def from_core(self, k, other_side):
        side = self.side + other_side - 2 * self.side * other_side
        shard = self.place(self.source(k), side, 1 - self.core)
        self.arrive(shard, self.core_peer(), (2 + other_side) * self.deep - 1 + k)

    def run(self, use):
        self.across_side(0)

        @pl.loop(0, 2 * self.deep)
        def _(turn):
            k, other = turn // 2, turn % 2

            @pl.when((k + 1 < self.deep) & (other == 0))
            def _():
                self.along_depth(k + 1)

            @pl.when((k + 1 < self.deep) & (other == 1))
            def _():
                self.across_side(k + 1)

            self.from_core(k, other)
            use(self.source(k), self.side + other - 2 * self.side * other)

    def wait_sent(self):
        own = self.place(self.depth, self.side, self.core)

        @pl.loop(0, 4 * self.deep - 1)
        def _(slot):
            for copy in self.copies(own, self.core_peer(), slot):
                copy.wait_send()


class StagedSum:
    def __init__(self, stages, sizes, part_ref, total_ref, landing, sems, rows):
        self.stages, self.sizes = stages, sizes
        self.part_ref, self.total_ref, self.landing, self.sems = part_ref, total_ref, landing, sems
        row = lax.axis_index("rows")
        self.me = {"z": row // 4, "x": (row // 2) % 2, "k": row % 2, "y": lax.axis_index("cols")}
        self.spans, base, size = [], 0, rows
        for stage in stages:
            size = size // members(stage, sizes)
            self.spans.append((base, size))
            base = base + self.number(self.me, stage) * size
        self.base, self.size = base, size
        self.unit = size

    def number(self, place, stage):
        out, scale = 0, 1
        for axis in stage:
            out = out + place[axis] * scale
            scale *= self.sizes[axis]
        return out

    def partner(self, stage, pattern):
        place = dict(self.me)
        for axis in stage:
            place[axis] = flip(self.me[axis], pattern % self.sizes[axis], self.sizes[axis])
            pattern //= self.sizes[axis]
        return place

    def device(self, place):
        return {"rows": (place["z"] * 2 + place["x"]) * 2 + place["k"], "cols": place["y"]}

    def rows_at(self, base, size):
        return pl.ds(pl.multiple_of(base, self.unit), size)

    def scatter(self, s):
        stage, (base, size) = self.stages[s], self.spans[s]
        found = []
        for j in range(1, members(stage, self.sizes)):
            place = self.partner(stage, j)
            rows = self.rows_at(base + self.number(place, stage) * size, size)
            found.append(
                pltpu.make_async_remote_copy(
                    src_ref=self.part_ref.at[rows, :],
                    dst_ref=self.landing[s].at[j - 1],
                    send_sem=self.sems.at[0, s, j - 1],
                    recv_sem=self.sems.at[1, s, j - 1],
                    device_id=self.device(place),
                    device_id_type=MESH,
                )
            )
        return found

    def scatter_start(self, s):
        for copy in self.scatter(s):
            copy.start()

    def scatter_finish(self, s):
        stage, (base, size) = self.stages[s], self.spans[s]
        rows = self.rows_at(base + self.number(self.me, stage) * size, size)
        total = self.part_ref[rows, :].astype(F32)
        copies = self.scatter(s)
        for j, copy in enumerate(copies):
            copy.wait_recv()
            total = total + self.landing[s][j].astype(F32)
        for copy in copies:
            copy.wait_send()
        target = self.total_ref if s == len(self.stages) - 1 else self.part_ref
        target[rows, :] = total.astype(BF16)

    def gather(self, s, own):
        stage, (base, size) = self.stages[s], self.spans[s]
        found = []
        for j in range(1, members(stage, self.sizes)):
            place = self.partner(stage, j)
            holder = self.me if own else place
            rows = self.rows_at(base + self.number(holder, stage) * size, size)
            found.append(
                pltpu.make_async_remote_copy(
                    src_ref=self.total_ref.at[rows, :],
                    dst_ref=self.total_ref.at[rows, :],
                    send_sem=self.sems.at[2, s, j - 1],
                    recv_sem=self.sems.at[3, s, j - 1],
                    device_id=self.device(place),
                    device_id_type=MESH,
                )
            )
        return found

    def gather_start(self, s):
        for copy in self.gather(s, True):
            copy.start()

    def gather_finish(self, s):
        for copy in self.gather(s, False):
            copy.wait_recv()
        for copy in self.gather(s, True):
            copy.wait_send()


def members(stage, sizes):
    return math.prod(sizes[axis] for axis in stage)


def meet(targets):
    barrier = pltpu.get_barrier_semaphore()
    for target in targets:
        pl.semaphore_signal(barrier, inc=1, device_id=target, device_id_type=MESH)
    pl.semaphore_wait(barrier, len(targets))


def swap_copy(source, landing, send_sem, recv_sem):
    return pltpu.make_async_remote_copy(
        src_ref=source,
        dst_ref=landing,
        send_sem=send_sem,
        recv_sem=recv_sem,
        device_id={"cols": 1 - lax.axis_index("cols")},
        device_id_type=MESH,
    )


def window_of(column, width, width_dev):
    start = (column * width) // LANES * LANES
    offset = column * width - start
    size = -(-(offset + width) // LANES) * LANES
    return start, offset, min(size, width_dev - start)


def padded_weight(weight, offset, size):
    width = weight.shape[1]
    parts = []
    if offset:
        parts.append(jnp.zeros((offset, width), F32))
    parts.append(weight)
    if size - offset - weight.shape[0]:
        parts.append(jnp.zeros((size - offset - weight.shape[0], width), F32))
    return (jnp.concatenate(parts, axis=0) if len(parts) > 1 else weight).astype(BF16)


def head_blocks(value, head_dim, offset=0, size=None):
    rows, width = value.shape
    if size is not None and size != width:
        parts = []
        if offset:
            parts.append(jnp.zeros((rows, offset), F32))
        parts.append(value)
        if size - offset - width:
            parts.append(jnp.zeros((rows, size - offset - width), F32))
        value = jnp.concatenate(parts, axis=1)
        width = size
    blocks = [
        jnp.where(head_mask(rows, width, head_dim, head, offset), value, 0.0).astype(BF16)
        for head in range(HEADS)
    ]
    return jnp.concatenate(blocks, axis=0)


def gather_heads(value, rows, head_dim, offset=0, width=None):
    total = None
    for head in range(HEADS):
        block = value[head * rows : (head + 1) * rows]
        kept = jnp.where(head_mask(rows, value.shape[1], head_dim, head, offset), block, 0.0)
        total = kept if total is None else total + kept
    if width is not None and width != total.shape[1]:
        total = total[:, offset : offset + width]
    return total


STAGES = ("k", "xy", "z")


def layer_kernel(
    rows_count,
    cols_count,
    train_ref,
    owner_ref,
    cells_ref,
    mask_ref,
    cotangent_ref,
    proj_ref,
    feat_out_ref,
    item_out_ref,
    mlp_in_ref,
    mlp_out_ref,
    gains_ref,
    shifts_ref,
    bank_first_ref,
    bank_second_ref,
    layer_ref,
    cells_grad_ref,
    early_total_ref,
    late_total_ref,
    sorted_ref,
    peer_ref,
    gathered_ref,
    keys_ref,
    values_ref,
    grads_ref,
    all_stats_ref,
    banks_ref,
    blocks_ref,
    grad_blocks_ref,
    wide_blocks_ref,
    top_ref,
    sum_ref,
    total_ref,
    value_total_ref,
    item_w_ref,
    branch_ref,
    peer_branch_ref,
    early_ref,
    late_ref,
    early_land_k,
    early_land_xy,
    early_land_z,
    late_land_k,
    late_land_xy,
    late_land_z,
    swap_sem,
    gather_sem,
    grads_sem,
    banks_sem,
    early_sem,
    late_sem,
):
    rows_dev, width_dev = cells_ref.shape
    width = feat_out_ref.shape[0]
    cols_dev = width_dev // width
    head_dim = width // HEADS
    scaling = head_dim ** (-0.5)
    ff_width = mlp_in_ref.shape[1]
    key_total = keys_ref.shape[1]
    chip_rows = 2 * rows_dev
    bank_slots = bank_first_ref.shape[0]
    train_count = train_ref[0]
    me = lax.axis_index("rows")
    sizes = {"z": rows_count // 4, "x": 2, "k": 2, "y": cols_count}
    own_count = cols_dev * rows_dev

    def shard_of(ref, rows):
        return lambda shard: ref.at[pl.ds(pl.multiple_of(shard * rows, rows), rows), :]

    def stats_shard(shard):
        return all_stats_ref.at[:, pl.ds(pl.multiple_of(shard * rows_dev, rows_dev), rows_dev)]

    hidden_gather = RowGather(
        [shard_of(gathered_ref, rows_dev)], gather_sem.at[0], gather_sem.at[1], rows_count
    )
    grads_gather = RowGather(
        [shard_of(grads_ref, rows_dev), stats_shard], grads_sem.at[0], grads_sem.at[1], rows_count
    )
    banks_gather = RowGather(
        [shard_of(banks_ref, bank_slots)], banks_sem.at[0], banks_sem.at[1], rows_count
    )
    early_sum = StagedSum(
        STAGES,
        sizes,
        early_ref,
        early_total_ref,
        (early_land_k, early_land_xy, early_land_z),
        early_sem,
        early_ref.shape[0],
    )
    late_sum = StagedSum(
        STAGES,
        sizes,
        late_ref,
        late_total_ref,
        (late_land_k, late_land_xy, late_land_z),
        late_sem,
        late_ref.shape[0],
    )
    meet(
        [
            early_sum.device(early_sum.partner(stage, j))
            for stage in STAGES
            for j in range(1, members(stage, sizes))
        ]
    )

    swap = swap_copy(cells_ref, peer_ref, swap_sem.at[0], swap_sem.at[1])
    swap.start()
    banks_ref[pl.ds(pl.multiple_of(me * bank_slots, bank_slots), bank_slots), :] = jnp.concatenate(
        [bank_first_ref[...], bank_second_ref[...]], axis=1
    ).astype(BF16)
    banks_gather.start_depth()
    feat_w = [proj_ref[n].astype(BF16) for n in range(3)]
    own = stack_columns(cells_ref[...].astype(F32), width)
    own_low = own.astype(BF16)
    queries, own_keys, own_values = [
        dot_nn(own_low, weight).astype(BF16).astype(F32) for weight in feat_w
    ]
    table = head_table(width, head_dim)
    wide = spread_table(width, head_dim)
    swap.wait()
    peer_low = stack_columns(peer_ref[...].astype(F32), width).astype(BF16)
    peer_queries, peer_keys, peer_values = [
        dot_nn(peer_low, weight).astype(BF16).astype(F32) for weight in feat_w
    ]
    feat_query = jnp.concatenate([queries, peer_queries], axis=0)
    all_keys = jnp.concatenate([own_keys, peer_keys], axis=0)
    all_values = jnp.concatenate([own_values, peer_values], axis=0)
    slots = all_keys.shape[0] // rows_dev
    own_first = lax.axis_index("cols") == 0
    key_list = [all_keys[n * rows_dev : (n + 1) * rows_dev] for n in range(slots)]
    value_list = [all_values[n * rows_dev : (n + 1) * rows_dev] for n in range(slots)]
    open_list = [column_open(mask_ref, own_first, cols_dev, n) for n in range(slots)]
    weights = feature_weights(feat_query, key_list, open_list, slots, table, scaling)
    mixed = None
    for weight, column_values in zip(weights, value_list):
        added = dot_nn(weight[:own_count].astype(BF16), wide) * tile_rows(column_values, cols_dev)
        mixed = added if mixed is None else mixed + added
    feat_mixed = mixed.astype(BF16)
    feat_out_w = feat_out_ref[...].astype(BF16)
    first_sum = own + dot_nn(feat_mixed, feat_out_w).astype(BF16).astype(F32)
    unit_one, root_one = norm_parts(first_sum)
    first_out = unit_one * gains_ref[0:1, :] + shifts_ref[0:1, :]
    first_low = first_out.astype(BF16)
    own_rows = pl.ds(pl.multiple_of(me * rows_dev, rows_dev), rows_dev)
    gathered_ref[own_rows, :] = pack_columns(first_out, rows_dev).astype(BF16)
    hidden_gather.start_near()
    hidden_gather.start_depth()

    item_w = [proj_ref[3 + n].astype(BF16) for n in range(3)]
    queries, own_keys, own_values = [
        dot_nn(first_low, weight).astype(BF16).astype(F32) for weight in item_w
    ]
    windows = [window_of(column, width, width_dev) for column in range(cols_dev)]
    for column, (_, offset, size) in enumerate(windows):
        for n in range(3):
            item_w_ref[column, n, 0:size, :] = padded_weight(proj_ref[3 + n], offset, size)
        blocks_ref[column] = head_blocks(
            queries[column * rows_dev : (column + 1) * rows_dev], head_dim
        )
    top_ref[...] = jnp.full(top_ref.shape, NEGATIVE, F32)
    sum_ref[...] = jnp.zeros(sum_ref.shape, F32)
    total_ref[...] = jnp.zeros(total_ref.shape, F32)

    def chip_start(depth, side):
        return pl.multiple_of((depth * 2 + side) * chip_rows, chip_rows)

    def masked_scores(column, keys, start_row):
        key_row = start_row + lax.broadcasted_iota(jnp.int32, (1, chip_rows), 1)
        scores = dot_nt(blocks_ref[column], keys) * scaling
        return jnp.where(key_row < train_count, scores, NEGATIVE)

    def attend_chip(depth, side):
        @pl.when(depth * 4 * rows_dev < key_total)
        def _():
            start_row = chip_start(depth, side)
            span = pl.ds(start_row, chip_rows)
            for column, (start, _, size) in enumerate(windows):
                hidden = gathered_ref[span, start : start + size]
                keys = dot_nn(hidden, item_w_ref[column, 1, 0:size, :]).astype(BF16)
                values = dot_nn(hidden, item_w_ref[column, 2, 0:size, :]).astype(BF16)
                keys_ref[column, span, :] = keys
                values_ref[column, span, :] = values
                scores = masked_scores(column, keys, start_row)
                top_old = top_ref[column]
                top_new = jnp.maximum(top_old, jnp.max(scores, axis=1, keepdims=True))
                grown = jnp.exp(scores - top_new)
                fade = jnp.exp(top_old - top_new)
                top_ref[column] = top_new
                sum_ref[column] = sum_ref[column] * fade + jnp.sum(grown, axis=1, keepdims=True)
                total_ref[column] = total_ref[column] * fade + dot_nn(grown.astype(BF16), values)

    hidden_gather.run(attend_chip)
    banks_gather.start_near()

    item_full, log_totals = [], []
    for column in range(cols_dev):
        item_full.append(gather_heads(total_ref[column] / sum_ref[column], rows_dev, head_dim))
        log_totals.append(top_ref[column] + jnp.log(sum_ref[column]))

    full = jnp.concatenate(item_full, axis=0)
    item_low = full.astype(BF16)
    item_out_w = item_out_ref[...].astype(BF16)
    mlp_in_w = mlp_in_ref[...].astype(BF16)
    mlp_out_w = mlp_out_ref[...].astype(BF16)
    unit_two, root_two = norm_parts(first_out + dot_nn(item_low, item_out_w))
    second_out = unit_two * gains_ref[1:2, :] + shifts_ref[1:2, :]
    second_low = second_out.astype(BF16)
    hidden_pre = dot_nn(second_low, mlp_in_w)
    normal = 0.5 + 0.5 * lax.erf(hidden_pre * (0.5**0.5))
    hidden_low = (hidden_pre * normal).astype(BF16)
    unit_three, root_three = norm_parts(second_out + dot_nt(hidden_low, mlp_out_w))
    third_out = unit_three * gains_ref[2:3, :] + shifts_ref[2:3, :]
    layer_ref[...] = pack_columns(third_out, rows_dev).astype(BF16)
    incoming = stack_columns(cotangent_ref[...].astype(F32), width)
    third_grad, gain_three, shift_three = norm_back(
        unit_three, root_three, gains_ref[2:3, :], incoming
    )
    branch_low = third_grad.astype(BF16)
    density = jnp.exp(-0.5 * hidden_pre * hidden_pre) * (1.0 / math.sqrt(2.0 * math.pi))
    pre_low = (dot_nn(branch_low, mlp_out_w) * (normal + hidden_pre * density)).astype(BF16)
    second_grad, gain_two, shift_two = norm_back(
        unit_two, root_two, gains_ref[1:2, :], third_grad + dot_nt(pre_low, mlp_in_w)
    )
    second_grad_low = second_grad.astype(BF16)
    mixed_grad = dot_nt(second_grad_low, item_out_w).astype(BF16).astype(F32)
    delta_all = head_sums(mixed_grad * full, table)
    lane = lax.broadcasted_iota(jnp.int32, (rows_dev, LANES), 1)
    deltas = []
    for column in range(cols_dev):
        rows_here = slice(column * rows_dev, (column + 1) * rows_dev)
        part = delta_all[rows_here]
        stat = jnp.zeros((rows_dev, LANES), F32)
        for head in range(HEADS):
            head_rows = slice(head * rows_dev, (head + 1) * rows_dev)
            stat = jnp.where(lane == head, log_totals[column][head_rows], stat)
            stat = jnp.where(lane == 8 + head, part[:, head : head + 1], stat)
        deltas.append(jnp.concatenate([part[:, h : h + 1] for h in range(HEADS)], axis=0))
        all_stats_ref[16 * column : 16 * (column + 1), own_rows] = jnp.transpose(stat)[0:16, :]
    grads_ref[own_rows, :] = pack_columns(mixed_grad, rows_dev).astype(BF16)
    grads_gather.start_near()
    grads_gather.start_depth()

    early_ref[2 * width : 3 * width, :] = dot_tn(second_low, pre_low).astype(BF16)
    early_ref[3 * width : 4 * width, :] = dot_tn(branch_low, hidden_low).astype(BF16)
    item_out_grad = dot_tn(item_low, second_grad_low)

    for column in range(cols_dev):
        rows_here = slice(column * rows_dev, (column + 1) * rows_dev)
        grad_blocks_ref[column] = head_blocks(mixed_grad[rows_here], head_dim)
    total_ref[...] = jnp.zeros(total_ref.shape, F32)

    @pl.loop(0, key_total // chip_rows)
    def _(step):
        start_row = pl.multiple_of(step * chip_rows, chip_rows)
        span = pl.ds(start_row, chip_rows)
        for column in range(cols_dev):
            keys = keys_ref[column, span, :]
            attend = jnp.exp(masked_scores(column, keys, start_row) - log_totals[column])
            dots = dot_nt(grad_blocks_ref[column], values_ref[column, span, :])
            score_grad = (attend * (dots - deltas[column])).astype(BF16)
            total_ref[column] += dot_nn(score_grad, keys)

    query_grads = [
        gather_heads(total_ref[column], rows_dev, head_dim) * scaling for column in range(cols_dev)
    ]

    own_row = me * rows_dev + lax.broadcasted_iota(jnp.int32, (rows_dev, 1), 0)
    own_open = own_row < train_count
    for column, (_, offset, size) in enumerate(windows):
        rows_here = slice(column * rows_dev, (column + 1) * rows_dev)
        blocks_ref[column] = head_blocks(own_keys[rows_here], head_dim)
        wide_blocks_ref[column, :, 0:size] = head_blocks(
            own_values[rows_here], head_dim, offset, size
        )
    total_ref[...] = jnp.zeros(total_ref.shape, F32)
    value_total_ref[...] = jnp.zeros(value_total_ref.shape, F32)

    def answer_chip(depth, side):
        span = pl.ds(chip_start(depth, side), chip_rows)
        for column, (start, _, size) in enumerate(windows):
            hidden = gathered_ref[span, start : start + size]
            asked = dot_nn(hidden, item_w_ref[column, 0, 0:size, :]).astype(BF16)
            grads = grads_ref[span, start : start + size]
            scores = dot_nt(blocks_ref[column], asked) * scaling
            dots = dot_nt(wide_blocks_ref[column, :, 0:size], grads)
            attends, score_grads = [], []
            for head in range(HEADS):
                part = slice(head * rows_dev, (head + 1) * rows_dev)
                log_total = all_stats_ref[16 * column + head : 16 * column + head + 1, span]
                delta = all_stats_ref[16 * column + 8 + head : 16 * column + 9 + head, span]
                attend = jnp.exp(jnp.where(own_open, scores[part], NEGATIVE) - log_total)
                attends.append(attend.astype(BF16))
                score_grads.append((attend * (dots[part] - delta)).astype(BF16))
            total_ref[column] += dot_nn(jnp.concatenate(score_grads, axis=0), asked)
            value_total_ref[column, :, 0:size] += dot_nn(jnp.concatenate(attends, axis=0), grads)

    grads_gather.run(answer_chip)

    key_grads, value_grads = [], []
    for column, (_, offset, size) in enumerate(windows):
        key_grads.append(gather_heads(total_ref[column], rows_dev, head_dim) * scaling)
        value_grads.append(
            gather_heads(value_total_ref[column, :, 0:size], rows_dev, head_dim, offset, width)
        )
    item_grads = [
        jnp.concatenate(parts, axis=0).astype(BF16)
        for parts in (query_grads, key_grads, value_grads)
    ]
    first_grad = second_grad
    for n in range(3):
        first_grad = first_grad + dot_nt(item_grads[n], item_w[n])
    first_in_grad, gain_one, shift_one = norm_back(
        unit_one, root_one, gains_ref[0:1, :], first_grad
    )
    branch_ref[...] = pack_columns(first_in_grad, rows_dev).astype(BF16)
    swap = swap_copy(branch_ref, peer_branch_ref, swap_sem.at[2], swap_sem.at[3])
    swap.start()

    def side_by_side(left, right):
        return jnp.concatenate([left, right], axis=1).astype(BF16)

    early_ref[0:width, :] = side_by_side(
        dot_tn(first_low, item_grads[0]), dot_tn(first_low, item_grads[1])
    )
    early_ref[width : 2 * width, :] = side_by_side(
        dot_tn(first_low, item_grads[2]), item_out_grad
    )
    if early_ref.shape[0] > 4 * width:
        early_ref[4 * width :, :] = jnp.zeros((early_ref.shape[0] - 4 * width, 2 * width), BF16)
    early_sum.scatter_start(0)
    banks_gather.across_side(0)
    for k in range(1, rows_count // 4):
        banks_gather.along_depth(k)
    early_sum.scatter_finish(0)
    early_sum.scatter_start(1)
    for k in range(1, rows_count // 4):
        banks_gather.across_side(k)

    own_branch = first_in_grad.astype(BF16)
    feat_out_grad = dot_tn(feat_mixed, own_branch)
    swap.wait()
    peer_branch = stack_columns(peer_branch_ref[...].astype(F32), width).astype(BF16)
    all_branch = jnp.concatenate([own_branch, peer_branch], axis=0)
    feat_grad = dot_nt(all_branch, feat_out_w).astype(BF16).astype(F32)
    dots = [head_sums(feat_grad * tile_rows(part, slots), table) for part in value_list]
    row_delta = None
    for weight, dot in zip(weights, dots):
        added = weight * dot
        row_delta = added if row_delta is None else row_delta + added
    score_grads = [
        (weight * (dot - row_delta)).astype(BF16) for weight, dot in zip(weights, dots)
    ]
    early_sum.scatter_finish(1)
    early_sum.scatter_start(2)
    query_grad = None
    for score_grad, part in zip(score_grads, key_list):
        added = dot_nn(score_grad[:own_count], wide) * tile_rows(part, cols_dev)
        query_grad = added if query_grad is None else query_grad + added
    key_parts, value_parts = [], []
    for column in range(cols_dev):
        key_products = dot_nn(score_grads[column], wide) * feat_query
        value_products = dot_nn(weights[column].astype(BF16), wide) * feat_grad
        key_sum = key_products[:rows_dev]
        value_sum = value_products[:rows_dev]
        for n in range(1, slots):
            key_sum = key_sum + key_products[n * rows_dev : (n + 1) * rows_dev]
            value_sum = value_sum + value_products[n * rows_dev : (n + 1) * rows_dev]
        key_parts.append(key_sum)
        value_parts.append(value_sum)
    feat_grads = [
        (query_grad * scaling).astype(BF16),
        (jnp.concatenate(key_parts, axis=0) * scaling).astype(BF16),
        jnp.concatenate(value_parts, axis=0).astype(BF16),
    ]
    late_ref[0:width, :] = side_by_side(
        dot_tn(own_low, feat_grads[0]), dot_tn(own_low, feat_grads[1])
    )
    late_ref[width : 2 * width, :] = side_by_side(dot_tn(own_low, feat_grads[2]), feat_out_grad)
    pairs = [
        jnp.concatenate(pair, axis=1)
        for pair in ((gain_one, shift_one), (gain_two, shift_two), (gain_three, shift_three))
    ]
    rest = late_ref.shape[0] - 2 * width - len(pairs)
    late_ref[2 * width :, :] = jnp.concatenate(
        pairs + [jnp.zeros((rest, 2 * width), F32)], axis=0
    ).astype(BF16)
    late_sum.scatter_start(0)
    early_sum.scatter_finish(2)
    early_sum.gather_start(2)
    late_sum.scatter_finish(0)
    late_sum.scatter_start(1)
    inner = None
    for n in range(3):
        added = dot_nt(feat_grads[n], feat_w[n])
        inner = added if inner is None else inner + added
    cells_grad_ref[...] = pack_columns(first_in_grad + inner.astype(BF16).astype(F32), rows_dev)
    for k in range(rows_count // 4):
        banks_gather.from_core(k, 0)
        banks_gather.from_core(k, 1)
    sort_rows = sorted_ref.shape[0]
    sort_block = math.gcd(sort_rows, 256)
    owner = owner_ref[...]

    def sort_some(first, last):
        @pl.loop(first, last)
        def _(step):
            start = pl.multiple_of(step * sort_block, sort_block)
            row = start + lax.broadcasted_iota(jnp.int32, (sort_block, sort_rows), 0)
            chosen = jnp.where(owner == row, 1.0, 0.0).astype(BF16)
            sorted_ref[pl.ds(start, sort_block), :] = dot_nn(chosen, banks_ref[...]).astype(BF16)

    thirds = sort_rows // sort_block // 3
    early_sum.gather_finish(2)
    early_sum.gather_start(1)
    late_sum.scatter_finish(1)
    late_sum.scatter_start(2)
    sort_some(0, thirds)
    early_sum.gather_finish(1)
    early_sum.gather_start(0)
    late_sum.scatter_finish(2)
    late_sum.gather_start(2)
    sort_some(thirds, 2 * thirds)
    late_sum.gather_finish(2)
    late_sum.gather_start(1)
    early_sum.gather_finish(0)
    sort_some(2 * thirds, sort_rows // sort_block)
    late_sum.gather_finish(1)
    late_sum.gather_start(0)
    for gather in (hidden_gather, grads_gather, banks_gather):
        gather.wait_sent()
    late_sum.gather_finish(0)


def moment_rule(gradient, first_old, second_old):
    first_new = BETA_ONE * first_old + (1.0 - BETA_ONE) * gradient
    second_new = BETA_TWO * second_old + (1.0 - BETA_TWO) * gradient * gradient
    first_hat = first_new * (1.0 / (1.0 - BETA_ONE**STEP))
    second_hat = second_new * (1.0 / (1.0 - BETA_TWO**STEP))
    return first_new, second_new, first_hat / (jnp.sqrt(second_hat) + EPSILON)


def root_mean(value):
    count = value.shape[0] * value.shape[1]
    square = jnp.sum(jnp.sum(value * value, axis=1, keepdims=True), axis=0, keepdims=True)
    return jnp.sqrt(square * (1.0 / count) + 1e-06)


def update_kernel(
    owner_ref,
    layer_ref,
    cells_grad_ref,
    early_ref,
    late_ref,
    sorted_ref,
    small_ref,
    big_ref,
    first_ref,
    second_ref,
    proj_ref,
    feat_out_ref,
    item_out_ref,
    mlp_in_ref,
    mlp_out_ref,
    gains_ref,
    shifts_ref,
    norm_first_ref,
    norm_second_ref,
    layer_out_ref,
    cells_out_ref,
    square_grad_ref,
    in_grad_ref,
    out_grad_ref,
    norm_grad_ref,
    clip_ref,
    first_new_ref,
    second_new_ref,
    square_new_ref,
    in_new_ref,
    out_new_ref,
    square_low_ref,
    in_low_ref,
    out_low_ref,
    norm_new_ref,
    norm_first_new_ref,
    norm_second_new_ref,
    rotated_ref,
    own_ref,
):
    width, ff_width = mlp_in_ref.shape
    slots = first_ref.shape[0]
    layer_out_ref[...] = layer_ref[...]
    cells_out_ref[...] = cells_grad_ref[...]

    early = early_ref[...].astype(F32)
    late = late_ref[...].astype(F32)
    square = None
    for part in (early, late):
        added = jnp.sum(jnp.sum(part * part, axis=1, keepdims=True), axis=0, keepdims=True)
        square = added if square is None else square + added
    grad_norm = jnp.sqrt(square)
    factor = jnp.minimum(1.0, CLIP_NORM / grad_norm)
    clip_ref[0] = grad_norm[0, 0]
    early = early * factor
    late = late * factor
    squares = [
        part[row : row + width, lane : lane + width]
        for part, row, lane in (
            (late, 0, 0),
            (late, 0, width),
            (late, width, 0),
            (early, 0, 0),
            (early, 0, width),
            (early, width, 0),
            (late, width, width),
            (early, width, width),
        )
    ]
    for n, clipped in enumerate(squares):
        square_grad_ref[n] = clipped
        turned = dot_fine(dot_nn, clipped, small_ref[8 + n])
        rotated_ref[n * width : (n + 1) * width, :] = dot_fine(dot_tn, small_ref[n], turned)
    start = len(squares) * width
    middle = start + ff_width
    clipped = early[2 * width : 3 * width]
    in_grad_ref[...] = clipped
    turned = dot_fine(dot_tn, clipped, small_ref[16])
    rotated_ref[start:middle, :] = dot_fine(dot_tn, big_ref[0], turned)
    clipped = early[3 * width : 4 * width]
    out_grad_ref[...] = clipped
    turned = dot_fine(dot_tn, clipped, small_ref[17])
    rotated_ref[middle : middle + ff_width, :] = dot_fine(dot_tn, big_ref[1], turned)

    base = lax.axis_index("rows") * slots

    @pl.loop(0, slots // 8)
    def _(step):
        for n in range(8):
            row = owner_ref[base + step * 8 + n]
            own_ref[pl.ds(step * 8 + n, 1), :] = rotated_ref[pl.ds(row, 1), :]

    first_new, second_new, _ = moment_rule(own_ref[...], first_ref[...], second_ref[...])
    first_new_ref[...] = first_new
    second_new_ref[...] = second_new

    def step_of(first_row, count):
        rows = slice(first_row, first_row + count)
        banks = sorted_ref[rows, :].astype(F32)
        return moment_rule(rotated_ref[rows, :], banks[:, :width], banks[:, width:])[2]

    for n in range(len(squares)):
        turned = dot_fine(dot_nt, step_of(n * width, width), small_ref[8 + n])
        update = dot_fine(dot_nn, small_ref[n], turned)
        old = proj_ref[n] if n < 6 else (feat_out_ref if n == 6 else item_out_ref)[...]
        new = old - LEARN_RATE * root_mean(old) * update
        square_new_ref[n] = new
        square_low_ref[n] = new.astype(BF16)
    turned = dot_fine(dot_nn, big_ref[0], step_of(start, ff_width))
    update = dot_fine(dot_nt, small_ref[16], turned)
    new = mlp_in_ref[...] - LEARN_RATE * root_mean(mlp_in_ref[...]) * update
    in_new_ref[...] = new
    in_low_ref[...] = new.astype(BF16)
    turned = dot_fine(dot_nn, big_ref[1], step_of(middle, ff_width))
    update = dot_fine(dot_nt, small_ref[17], turned)
    new = mlp_out_ref[...] - LEARN_RATE * root_mean(mlp_out_ref[...]) * update
    out_new_ref[...] = new
    out_low_ref[...] = new.astype(BF16)

    for n in range(3):
        pair = late[2 * width + n : 2 * width + n + 1]
        both = jnp.concatenate([pair[:, :width], pair[:, width:]], axis=0)
        norm_grad_ref[n] = both
        first_new, second_new, change = moment_rule(both, norm_first_ref[n], norm_second_ref[n])
        norm_first_new_ref[n] = first_new
        norm_second_new_ref[n] = second_new
        old = jnp.concatenate([gains_ref[n : n + 1, :], shifts_ref[n : n + 1, :]], axis=0)
        size = jnp.sqrt(jnp.sum(old * old, axis=1, keepdims=True) * (1.0 / width) + 1e-06)
        norm_new_ref[n] = old - LEARN_RATE * size * change


def in_vmem():
    return pl.BlockSpec(memory_space=pltpu.VMEM)


def in_smem():
    return pl.BlockSpec(memory_space=pltpu.SMEM)


def fast_device(
    cells,
    feat_mask,
    train_rows,
    cotangent,
    proj_weights,
    feat_out_w,
    item_out_w,
    mlp_in,
    mlp_out,
    norm_gains,
    norm_shifts,
    bases_small,
    bases_big,
    owner_rows,
    bank_first,
    bank_second,
    norm_first,
    norm_second,
):
    rows_count, cols_count = lax.axis_size("rows"), lax.axis_size("cols")
    rows_dev, width_dev = cells.shape
    width = proj_weights.shape[-1]
    cols_dev = width_dev // width
    rows_all = rows_dev * rows_count
    key_total = rows_all // 4 * 3
    head_rows = HEADS * rows_dev
    slots = RowGather.slots(rows_count)
    dma = pltpu.SemaphoreType.DMA
    shape = jax.ShapeDtypeStruct
    devices = rows_count * cols_count
    sizes = {"z": rows_count // 4, "x": 2, "k": 2, "y": cols_count}

    mask_rows = feat_mask.T
    mlp_out_turned = mlp_out.T
    norm_first_turned = jnp.transpose(norm_first, (1, 0, 2))
    norm_second_turned = jnp.transpose(norm_second, (1, 0, 2))
    bank_rows = owner_rows.shape[0]

    def block_rows(rows):
        return -(-rows // (16 * devices)) * 16 * devices

    def landings(rows):
        found = []
        for stage in STAGES:
            count = members(stage, sizes)
            rows //= count
            found.append(pltpu.VMEM((count - 1, rows, 2 * width), BF16))
        return found

    early_rows = block_rows(4 * width)
    late_rows = block_rows(2 * width + 3)
    widest = max(members(stage, sizes) for stage in STAGES) - 1
    layer_part, cells_part, early_total, late_total, sorted_banks = pl.pallas_call(
        functools.partial(layer_kernel, rows_count, cols_count),
        name="layer_and_gradients",
        out_shape=(
            shape((rows_dev, width_dev), BF16),
            shape((rows_dev, width_dev), F32),
            shape((early_rows, 2 * width), BF16),
            shape((late_rows, 2 * width), BF16),
            shape((bank_rows, 2 * width), BF16),
        ),
        in_specs=[in_smem()] + [in_vmem()] * 13,
        out_specs=[in_vmem()] * 5,
        scratch_shapes=[
            pltpu.VMEM((rows_dev, width_dev), BF16),
            pltpu.VMEM((rows_all, width_dev), BF16),
            pltpu.VMEM((cols_dev, key_total, width), BF16),
            pltpu.VMEM((cols_dev, key_total, width), BF16),
            pltpu.VMEM((rows_all, width_dev), BF16),
            pltpu.VMEM((16 * cols_dev, rows_all), F32),
            pltpu.VMEM((bank_rows, 2 * width), BF16),
            pltpu.VMEM((cols_dev, head_rows, width), BF16),
            pltpu.VMEM((cols_dev, head_rows, width), BF16),
            pltpu.VMEM((cols_dev, head_rows, 2 * LANES), BF16),
            pltpu.VMEM((cols_dev, head_rows, 1), F32),
            pltpu.VMEM((cols_dev, head_rows, 1), F32),
            pltpu.VMEM((cols_dev, head_rows, width), F32),
            pltpu.VMEM((cols_dev, head_rows, 2 * LANES), F32),
            pltpu.VMEM((cols_dev, 3, 2 * LANES, width), BF16),
            pltpu.VMEM((rows_dev, width_dev), BF16),
            pltpu.VMEM((rows_dev, width_dev), BF16),
            pltpu.VMEM((early_rows, 2 * width), BF16),
            pltpu.VMEM((late_rows, 2 * width), BF16),
        ]
        + landings(early_rows)
        + landings(late_rows)
        + [
            dma((4,)),
            dma((2, 1, slots)),
            dma((2, 2, slots)),
            dma((2, 1, slots)),
            dma((4, len(STAGES), widest)),
            dma((4, len(STAGES), widest)),
        ],
        compiler_params=pltpu.CompilerParams(
            collective_id=0, has_side_effects=True, vmem_limit_bytes=VMEM_BYTES
        ),
    )(
        train_rows,
        owner_rows.reshape(1, bank_rows),
        cells,
        mask_rows,
        cotangent,
        proj_weights,
        feat_out_w,
        item_out_w,
        mlp_in,
        mlp_out_turned,
        norm_gains,
        norm_shifts,
        bank_first,
        bank_second,
    )

    slots_dev = bank_first.shape[0]
    square = (8, width, width)
    (
        layer_out,
        cells_grad,
        square_grads,
        in_grad,
        out_grad,
        norm_grads,
        clip_norm,
        first_new,
        second_new,
        square_new,
        in_new,
        out_new,
        square_low,
        in_low,
        out_low,
        norm_new,
        norm_first_new,
        norm_second_new,
    ) = pl.pallas_call(
        update_kernel,
        name="rotated_update",
        out_shape=(
            shape(layer_part.shape, BF16),
            shape(cells_part.shape, F32),
            shape(square, F32),
            shape(mlp_in.shape, F32),
            shape(mlp_in.shape, F32),
            shape(norm_first_turned.shape, F32),
            shape((1,), F32),
            shape(bank_first.shape, F32),
            shape(bank_first.shape, F32),
            shape(square, F32),
            shape(mlp_in.shape, F32),
            shape(mlp_in.shape, F32),
            shape(square, BF16),
            shape(mlp_in.shape, BF16),
            shape(mlp_in.shape, BF16),
            shape(norm_first_turned.shape, F32),
            shape(norm_first_turned.shape, F32),
            shape(norm_first_turned.shape, F32),
        ),
        in_specs=[in_smem()] + [in_vmem()] * 18,
        out_specs=[in_vmem()] * 6 + [in_smem()] + [in_vmem()] * 11,
        scratch_shapes=[
            pltpu.VMEM((bank_rows, width), F32),
            pltpu.VMEM((slots_dev, width), F32),
        ],
        compiler_params=pltpu.CompilerParams(vmem_limit_bytes=VMEM_BYTES),
    )(
        owner_rows,
        layer_part,
        cells_part,
        early_total,
        late_total,
        sorted_banks,
        bases_small,
        bases_big,
        bank_first,
        bank_second,
        proj_weights,
        feat_out_w,
        item_out_w,
        mlp_in,
        mlp_out_turned,
        norm_gains,
        norm_shifts,
        norm_first_turned,
        norm_second_turned,
    )
    return (
        layer_out,
        cells_grad,
        square_grads,
        in_grad,
        out_grad.T,
        jnp.transpose(norm_grads, (1, 0, 2)),
        clip_norm,
        first_new,
        second_new,
        square_new,
        in_new,
        out_new.T,
        square_low,
        in_low,
        out_low.T,
        jnp.transpose(norm_new, (1, 0, 2)),
        jnp.transpose(norm_first_new, (1, 0, 2)),
        jnp.transpose(norm_second_new, (1, 0, 2)),
    )


def solution(mesh):
    in_specs = (
        P("rows", "cols"),
        P("rows", None),
        P(),
        P("rows", "cols"),
        P(),
        P(),
        P(),
        P(),
        P(),
        P(),
        P(),
        P(),
        P(),
        P(),
        P("rows", None),
        P("rows", None),
        P(),
        P(),
    )
    out_specs = (
        P("rows", "cols"),
        P("rows", "cols"),
        P(),
        P(),
        P(),
        P(),
        P(),
        P("rows", None),
        P("rows", None),
        P(),
        P(),
        P(),
        P(),
        P(),
        P(),
        P(),
        P(),
        P(),
    )
    small = mesh.shape["rows"] == 16 and mesh.shape["cols"] == 2
    return jax.shard_map(
        fast_device if small else per_device, mesh=mesh, in_specs=in_specs, out_specs=out_specs, check_vma=False
    )
```

profile of v0, /device:TPU:0, one launch (start us, length us, event | category | flops | bytes accessed | tf_op | source)
XLA Modules:
  0.0 133.2 jit_solution(13436302775005219590)
XLA Ops:
  1.3 1.3 reshape.39.owner_ref
  2.6 116.5 %layer_and_gradients.1 = (bf16[128,384]{1,0:T(8,128)(2,1)}, f32[128,384]{1,0:T(8,128)}, bf16[1024,384]{1,0:T(8,128)(2,1)}, bf16[512,384]{1,0:T(8,128)(2,1)}, bf16[2304,384]{1,0:T(8,128)(2,1)}) custom-call(s32[1]{0:T(128)S(6)} %copy.36.train_ref, s32[1,2304]{1,0:T(1,128)} %reshape.39.owner_ref, bf16[128,384]{1,0:T(8,128)(2,1)} %cells_ref.1, ...), custom_call_target="tpu_custom_call" | custom-call | tf_op jit(solution)/shard_map/layer_and_gradients/pallas_call | solution.py:1518
  119.1 13.9 %rotated_update.1 = (bf16[128,384]{1,0:T(8,128)(2,1)}, f32[128,384]{1,0:T(8,128)}, f32[8,192,192]{2,1,0:T(8,128)}, f32[192,384]{1,0:T(8,128)}, f32[192,384]{1,0:...) custom-call(s32[2304]{0:T(1024)} %owner_ref.1, ...), custom_call_target="tpu_custom_call" | custom-call | tf_op jit(solution)/shard_map/rotated_update/pallas_call | solution.py:1602
where the time goes:
time: 133 us
  Pallas kernels  130 us (98%)
  between operations  1.49 us (1%)
    pallas_call x1, Pallas kernels, fast_device(): pl.pallas_call(functools.partial(layer_kernel, rows_count, cols_count), n...  116 us
    pallas_call x1, Pallas kernels, fast_device(): pl.pallas_call(update_kernel, name='rotated_update', out_shape=(shape(lay...  13.9 us

commit v1 on v0

--- a/solution.py
+++ b/solution.py
@@ -506,10 +506,8 @@
     return high, (value - high.astype(F32)).astype(BF16)
 
 
-def dot_fine(dot, left, right):
-    left_high, left_low = split_two(left)
-    right_high, right_low = split_two(right)
-    return dot(left_high, right_high) + (dot(left_high, right_low) + dot(left_low, right_high))
+def dot_low(dot, left, right):
+    return dot(left.astype(BF16), right.astype(BF16))
 
 
 def stack_columns(packed, width):
@@ -553,6 +551,11 @@
     feature = lax.broadcasted_iota(jnp.int32, (LANES, width), 1)
     inside = (feature >= head * head_dim) & (feature < (head + 1) * head_dim)
     return jnp.where(inside, 1.0, 0.0).astype(BF16)
+
+
+def head_rows_of(value, wide):
+    high, low = split_two(value)
+    return dot_nt(wide, high) + dot_nt(wide, low)
 
 
 def head_sums(value, table):
@@ -701,12 +704,12 @@
 
 
 class StagedSum:
-    def __init__(self, stages, sizes, part_ref, total_ref, landing, sems, rows):
+    def __init__(self, stages, sizes, part_ref, total_ref, landing, sems):
         self.stages, self.sizes = stages, sizes
         self.part_ref, self.total_ref, self.landing, self.sems = part_ref, total_ref, landing, sems
         row = lax.axis_index("rows")
         self.me = {"z": row // 4, "x": (row // 2) % 2, "k": row % 2, "y": lax.axis_index("cols")}
-        self.spans, base, size = [], 0, rows
+        self.spans, base, size = [], 0, part_ref.shape[0]
         for stage in stages:
             size = size // members(stage, sizes)
             self.spans.append((base, size))
@@ -799,6 +802,39 @@
             copy.wait_send()
 
 
+class Mover:
+    def __init__(self, sem):
+        self.sem, self.count = sem, 0
+
+    def start(self, source, target):
+        copy = pltpu.make_async_copy(source, target, self.sem.at[self.count])
+        copy.start()
+        self.count += 1
+        return copy
+
+
+def put_tiles(ref, row, value):
+    rows, lanes = value.shape
+    if lanes % LANES:
+        value = jnp.concatenate([value, jnp.zeros((rows, LANES - lanes % LANES), F32)], axis=1)
+    for n in range(value.shape[1] // LANES):
+        ref[row : row + rows, :] = value[:, n * LANES : (n + 1) * LANES].astype(ref.dtype)
+        row += rows
+    return row
+
+
+def put_zeros(ref, row):
+    if row < ref.shape[0]:
+        ref[row:, :] = jnp.zeros((ref.shape[0] - row, ref.shape[1]), ref.dtype)
+
+
+def take_tiles(ref, row, rows, lanes):
+    count = -(-lanes // LANES)
+    tiles = [ref[row + n * rows : row + (n + 1) * rows, :].astype(F32) for n in range(count)]
+    value = jnp.concatenate(tiles, axis=1)
+    return value if lanes % LANES == 0 else value[:, :lanes]
+
+
 def members(stage, sizes):
     return math.prod(sizes[axis] for axis in stage)
 
@@ -837,6 +873,17 @@
     if size - offset - weight.shape[0]:
         parts.append(jnp.zeros((size - offset - weight.shape[0], width), F32))
     return (jnp.concatenate(parts, axis=0) if len(parts) > 1 else weight).astype(BF16)
+
+
+def padded_turned(weight, offset, size):
+    width = weight.shape[0]
+    parts = []
+    if offset:
+        parts.append(jnp.zeros((width, offset), F32))
+    parts.append(jnp.transpose(weight))
+    if size - offset - width:
+        parts.append(jnp.zeros((width, size - offset - width), F32))
+    return (jnp.concatenate(parts, axis=1) if len(parts) > 1 else parts[0]).astype(BF16)
 
 
 def head_blocks(value, head_dim, offset=0, size=None):
@@ -857,6 +904,14 @@
     return jnp.concatenate(blocks, axis=0)
 
 
+def gather_heads_turned(value, rows, head_dim):
+    blocks = [
+        value[head * head_dim : (head + 1) * head_dim, head * rows : (head + 1) * rows]
+        for head in range(HEADS)
+    ]
+    return jnp.transpose(jnp.concatenate(blocks, axis=0))
+
+
 def gather_heads(value, rows, head_dim, offset=0, width=None):
     total = None
     for head in range(HEADS):
@@ -878,24 +933,37 @@
     owner_ref,
     cells_ref,
     mask_ref,
-    cotangent_ref,
+    gains_ref,
+    shifts_ref,
+    proj_in,
+    feat_out_in,
+    bank_first_in,
+    bank_second_in,
+    item_out_in,
+    mlp_in_in,
+    mlp_out_in,
+    cotangent_in,
+    layer_out,
+    cells_grad_out,
+    mlp_total_ref,
+    item_total_ref,
+    feat_total_ref,
+    sorted_out,
     proj_ref,
     feat_out_ref,
+    bank_first_ref,
+    bank_second_ref,
     item_out_ref,
     mlp_in_ref,
     mlp_out_ref,
-    gains_ref,
-    shifts_ref,
-    bank_first_ref,
-    bank_second_ref,
+    cotangent_ref,
     layer_ref,
     cells_grad_ref,
-    early_total_ref,
-    late_total_ref,
     sorted_ref,
     peer_ref,
     gathered_ref,
     keys_ref,
+    keys_turned_ref,
     values_ref,
     grads_ref,
     all_stats_ref,
@@ -905,26 +973,50 @@
     wide_blocks_ref,
     top_ref,
     sum_ref,
+    turned_ref,
     total_ref,
     value_total_ref,
     item_w_ref,
+    item_turned_ref,
     branch_ref,
     peer_branch_ref,
-    early_ref,
-    late_ref,
-    early_land_k,
-    early_land_xy,
-    early_land_z,
-    late_land_k,
-    late_land_xy,
-    late_land_z,
+    mlp_part_ref,
+    item_part_ref,
+    feat_part_ref,
+    mlp_land_k,
+    mlp_land_xy,
+    mlp_land_z,
+    item_land_k,
+    item_land_xy,
+    item_land_z,
+    feat_land_k,
+    feat_land_xy,
+    feat_land_z,
     swap_sem,
     gather_sem,
     grads_sem,
     banks_sem,
-    early_sem,
-    late_sem,
+    mlp_sem,
+    item_sem,
+    feat_sem,
+    move_sem,
 ):
+    mover = Mover(move_sem)
+    proj_load = mover.start(proj_in, proj_ref)
+    feat_out_load = mover.start(feat_out_in, feat_out_ref)
+    bank_loads = [
+        mover.start(bank_first_in, bank_first_ref),
+        mover.start(bank_second_in, bank_second_ref),
+    ]
+    later_loads = [
+        mover.start(source, target)
+        for source, target in (
+            (item_out_in, item_out_ref),
+            (mlp_in_in, mlp_in_ref),
+            (mlp_out_in, mlp_out_ref),
+            (cotangent_in, cotangent_ref),
+        )
+    ]
     rows_dev, width_dev = cells_ref.shape
     width = feat_out_ref.shape[0]
     cols_dev = width_dev // width
@@ -954,27 +1046,33 @@
     banks_gather = RowGather(
         [shard_of(banks_ref, bank_slots)], banks_sem.at[0], banks_sem.at[1], rows_count
     )
-    early_sum = StagedSum(
+    mlp_sum = StagedSum(
         STAGES,
         sizes,
-        early_ref,
-        early_total_ref,
-        (early_land_k, early_land_xy, early_land_z),
-        early_sem,
-        early_ref.shape[0],
-    )
-    late_sum = StagedSum(
+        mlp_part_ref,
+        mlp_total_ref,
+        (mlp_land_k, mlp_land_xy, mlp_land_z),
+        mlp_sem,
+    )
+    item_sum = StagedSum(
         STAGES,
         sizes,
-        late_ref,
-        late_total_ref,
-        (late_land_k, late_land_xy, late_land_z),
-        late_sem,
-        late_ref.shape[0],
+        item_part_ref,
+        item_total_ref,
+        (item_land_k, item_land_xy, item_land_z),
+        item_sem,
+    )
+    feat_sum = StagedSum(
+        STAGES,
+        sizes,
+        feat_part_ref,
+        feat_total_ref,
+        (feat_land_k, feat_land_xy, feat_land_z),
+        feat_sem,
     )
     meet(
         [
-            early_sum.device(early_sum.partner(stage, j))
+            mlp_sum.device(mlp_sum.partner(stage, j))
             for stage in STAGES
             for j in range(1, members(stage, sizes))
         ]
@@ -982,10 +1080,14 @@
 
     swap = swap_copy(cells_ref, peer_ref, swap_sem.at[0], swap_sem.at[1])
     swap.start()
+    for load in bank_loads:
+        load.wait()
     banks_ref[pl.ds(pl.multiple_of(me * bank_slots, bank_slots), bank_slots), :] = jnp.concatenate(
         [bank_first_ref[...], bank_second_ref[...]], axis=1
     ).astype(BF16)
+    banks_gather.start_near()
     banks_gather.start_depth()
+    proj_load.wait()
     feat_w = [proj_ref[n].astype(BF16) for n in range(3)]
     own = stack_columns(cells_ref[...].astype(F32), width)
     own_low = own.astype(BF16)
@@ -1013,6 +1115,7 @@
         added = dot_nn(weight[:own_count].astype(BF16), wide) * tile_rows(column_values, cols_dev)
         mixed = added if mixed is None else mixed + added
     feat_mixed = mixed.astype(BF16)
+    feat_out_load.wait()
     feat_out_w = feat_out_ref[...].astype(BF16)
     first_sum = own + dot_nn(feat_mixed, feat_out_w).astype(BF16).astype(F32)
     unit_one, root_one = norm_parts(first_sum)
@@ -1031,20 +1134,23 @@
     for column, (_, offset, size) in enumerate(windows):
         for n in range(3):
             item_w_ref[column, n, 0:size, :] = padded_weight(proj_ref[3 + n], offset, size)
+        for n in range(2):
+            item_turned_ref[column, n, :, 0:size] = padded_turned(proj_ref[4 + n], offset, size)
         blocks_ref[column] = head_blocks(
             queries[column * rows_dev : (column + 1) * rows_dev], head_dim
         )
     top_ref[...] = jnp.full(top_ref.shape, NEGATIVE, F32)
     sum_ref[...] = jnp.zeros(sum_ref.shape, F32)
-    total_ref[...] = jnp.zeros(total_ref.shape, F32)
+    turned_ref[...] = jnp.zeros(turned_ref.shape, F32)
+    to_log2 = scaling * math.log2(math.e)
 
     def chip_start(depth, side):
         return pl.multiple_of((depth * 2 + side) * chip_rows, chip_rows)
 
     def masked_scores(column, keys, start_row):
-        key_row = start_row + lax.broadcasted_iota(jnp.int32, (1, chip_rows), 1)
-        scores = dot_nt(blocks_ref[column], keys) * scaling
-        return jnp.where(key_row < train_count, scores, NEGATIVE)
+        raw = dot_nt(keys, blocks_ref[column]) * to_log2
+        key_row = lax.broadcasted_iota(jnp.int32, raw.shape, 0)
+        return jnp.where(key_row < train_count - start_row, raw, NEGATIVE)
 
     def attend_chip(depth, side):
         @pl.when(depth * 4 * rows_dev < key_total)
@@ -1054,28 +1160,40 @@
             for column, (start, _, size) in enumerate(windows):
                 hidden = gathered_ref[span, start : start + size]
                 keys = dot_nn(hidden, item_w_ref[column, 1, 0:size, :]).astype(BF16)
-                values = dot_nn(hidden, item_w_ref[column, 2, 0:size, :]).astype(BF16)
                 keys_ref[column, span, :] = keys
-                values_ref[column, span, :] = values
+                values_ref[column, span, :] = dot_nn(
+                    hidden, item_w_ref[column, 2, 0:size, :]
+                ).astype(BF16)
+                keys_turned_ref[column, :, span] = dot_nt(
+                    item_turned_ref[column, 0, :, 0:size], hidden
+                ).astype(BF16)
+                values_turned = dot_nt(item_turned_ref[column, 1, :, 0:size], hidden).astype(BF16)
                 scores = masked_scores(column, keys, start_row)
                 top_old = top_ref[column]
-                top_new = jnp.maximum(top_old, jnp.max(scores, axis=1, keepdims=True))
-                grown = jnp.exp(scores - top_new)
-                fade = jnp.exp(top_old - top_new)
+                top_new = jnp.maximum(top_old, jnp.max(scores, axis=0, keepdims=True))
+                grown = jnp.exp2(scores - top_new)
+                fade = jnp.exp2(top_old - top_new)
                 top_ref[column] = top_new
-                sum_ref[column] = sum_ref[column] * fade + jnp.sum(grown, axis=1, keepdims=True)
-                total_ref[column] = total_ref[column] * fade + dot_nn(grown.astype(BF16), values)
+                sum_ref[column] = sum_ref[column] * fade + jnp.sum(grown, axis=0, keepdims=True)
+                turned_ref[column] = turned_ref[column] * fade + dot_nn(
+                    values_turned, grown.astype(BF16)
+                )
 
     hidden_gather.run(attend_chip)
-    banks_gather.start_near()
+    for k in range(1, rows_count // 4):
+        banks_gather.along_depth(k)
 
     item_full, log_totals = [], []
     for column in range(cols_dev):
-        item_full.append(gather_heads(total_ref[column] / sum_ref[column], rows_dev, head_dim))
-        log_totals.append(top_ref[column] + jnp.log(sum_ref[column]))
+        item_full.append(
+            gather_heads_turned(turned_ref[column] / sum_ref[column], rows_dev, head_dim)
+        )
+        log_totals.append(top_ref[column] + jnp.log2(sum_ref[column]))
 
     full = jnp.concatenate(item_full, axis=0)
     item_low = full.astype(BF16)
+    for load in later_loads:
+        load.wait()
     item_out_w = item_out_ref[...].astype(BF16)
     mlp_in_w = mlp_in_ref[...].astype(BF16)
     mlp_out_w = mlp_out_ref[...].astype(BF16)
@@ -1088,6 +1206,7 @@
     unit_three, root_three = norm_parts(second_out + dot_nt(hidden_low, mlp_out_w))
     third_out = unit_three * gains_ref[2:3, :] + shifts_ref[2:3, :]
     layer_ref[...] = pack_columns(third_out, rows_dev).astype(BF16)
+    results = [mover.start(layer_ref, layer_out)]
     incoming = stack_columns(cotangent_ref[...].astype(F32), width)
     third_grad, gain_three, shift_three = norm_back(
         unit_three, root_three, gains_ref[2:3, :], incoming
@@ -1100,31 +1219,34 @@
     )
     second_grad_low = second_grad.astype(BF16)
     mixed_grad = dot_nt(second_grad_low, item_out_w).astype(BF16).astype(F32)
-    delta_all = head_sums(mixed_grad * full, table)
-    lane = lax.broadcasted_iota(jnp.int32, (rows_dev, LANES), 1)
+    delta_all = head_rows_of(mixed_grad * full, wide)
     deltas = []
+    spare = jnp.zeros((8 - HEADS, rows_dev), F32)
     for column in range(cols_dev):
-        rows_here = slice(column * rows_dev, (column + 1) * rows_dev)
-        part = delta_all[rows_here]
-        stat = jnp.zeros((rows_dev, LANES), F32)
-        for head in range(HEADS):
-            head_rows = slice(head * rows_dev, (head + 1) * rows_dev)
-            stat = jnp.where(lane == head, log_totals[column][head_rows], stat)
-            stat = jnp.where(lane == 8 + head, part[:, head : head + 1], stat)
-        deltas.append(jnp.concatenate([part[:, h : h + 1] for h in range(HEADS)], axis=0))
-        all_stats_ref[16 * column : 16 * (column + 1), own_rows] = jnp.transpose(stat)[0:16, :]
+        part = delta_all[0:8, column * rows_dev : (column + 1) * rows_dev]
+        deltas.append(jnp.concatenate([part[h : h + 1] for h in range(HEADS)], axis=1))
+        totals = [
+            log_totals[column][:, head * rows_dev : (head + 1) * rows_dev]
+            for head in range(HEADS)
+        ]
+        all_stats_ref[16 * column : 16 * column + 8, own_rows] = jnp.concatenate(
+            totals + [spare], axis=0
+        )
+        all_stats_ref[16 * column + 8 : 16 * column + 16, own_rows] = part
     grads_ref[own_rows, :] = pack_columns(mixed_grad, rows_dev).astype(BF16)
     grads_gather.start_near()
     grads_gather.start_depth()
 
-    early_ref[2 * width : 3 * width, :] = dot_tn(second_low, pre_low).astype(BF16)
-    early_ref[3 * width : 4 * width, :] = dot_tn(branch_low, hidden_low).astype(BF16)
-    item_out_grad = dot_tn(item_low, second_grad_low)
+    row = put_tiles(mlp_part_ref, 0, dot_tn(second_low, pre_low))
+    row = put_tiles(mlp_part_ref, row, dot_tn(branch_low, hidden_low))
+    row = put_tiles(mlp_part_ref, row, dot_tn(item_low, second_grad_low))
+    put_zeros(mlp_part_ref, row)
+    mlp_sum.scatter_start(0)
 
     for column in range(cols_dev):
         rows_here = slice(column * rows_dev, (column + 1) * rows_dev)
         grad_blocks_ref[column] = head_blocks(mixed_grad[rows_here], head_dim)
-    total_ref[...] = jnp.zeros(total_ref.shape, F32)
+    turned_ref[...] = jnp.zeros(turned_ref.shape, F32)
 
     @pl.loop(0, key_total // chip_rows)
     def _(step):
@@ -1132,17 +1254,20 @@
         span = pl.ds(start_row, chip_rows)
         for column in range(cols_dev):
             keys = keys_ref[column, span, :]
-            attend = jnp.exp(masked_scores(column, keys, start_row) - log_totals[column])
-            dots = dot_nt(grad_blocks_ref[column], values_ref[column, span, :])
+            attend = jnp.exp2(masked_scores(column, keys, start_row) - log_totals[column])
+            dots = dot_nt(values_ref[column, span, :], grad_blocks_ref[column])
             score_grad = (attend * (dots - deltas[column])).astype(BF16)
-            total_ref[column] += dot_nn(score_grad, keys)
+            turned_ref[column] += dot_nn(keys_turned_ref[column, :, span], score_grad)
 
     query_grads = [
-        gather_heads(total_ref[column], rows_dev, head_dim) * scaling for column in range(cols_dev)
+        gather_heads_turned(turned_ref[column], rows_dev, head_dim) * scaling
+        for column in range(cols_dev)
     ]
-
-    own_row = me * rows_dev + lax.broadcasted_iota(jnp.int32, (rows_dev, 1), 0)
-    own_open = own_row < train_count
+    mlp_sum.scatter_finish(0)
+    mlp_sum.scatter_start(1)
+    for k in range(rows_count // 4):
+        banks_gather.across_side(k)
+
     for column, (_, offset, size) in enumerate(windows):
         rows_here = slice(column * rows_dev, (column + 1) * rows_dev)
         blocks_ref[column] = head_blocks(own_keys[rows_here], head_dim)
@@ -1158,27 +1283,33 @@
             hidden = gathered_ref[span, start : start + size]
             asked = dot_nn(hidden, item_w_ref[column, 0, 0:size, :]).astype(BF16)
             grads = grads_ref[span, start : start + size]
-            scores = dot_nt(blocks_ref[column], asked) * scaling
+            scores = dot_nt(blocks_ref[column], asked) * to_log2
             dots = dot_nt(wide_blocks_ref[column, :, 0:size], grads)
             attends, score_grads = [], []
             for head in range(HEADS):
                 part = slice(head * rows_dev, (head + 1) * rows_dev)
                 log_total = all_stats_ref[16 * column + head : 16 * column + head + 1, span]
                 delta = all_stats_ref[16 * column + 8 + head : 16 * column + 9 + head, span]
-                attend = jnp.exp(jnp.where(own_open, scores[part], NEGATIVE) - log_total)
+                attend = jnp.exp2(scores[part] - log_total)
                 attends.append(attend.astype(BF16))
                 score_grads.append((attend * (dots[part] - delta)).astype(BF16))
             total_ref[column] += dot_nn(jnp.concatenate(score_grads, axis=0), asked)
             value_total_ref[column, :, 0:size] += dot_nn(jnp.concatenate(attends, axis=0), grads)
 
     grads_gather.run(answer_chip)
-
+    mlp_sum.scatter_finish(1)
+    mlp_sum.scatter_start(2)
+
+    own_row = me * rows_dev + lax.broadcasted_iota(jnp.int32, (rows_dev, width), 0)
+    own_open = own_row < train_count
     key_grads, value_grads = [], []
     for column, (_, offset, size) in enumerate(windows):
-        key_grads.append(gather_heads(total_ref[column], rows_dev, head_dim) * scaling)
-        value_grads.append(
-            gather_heads(value_total_ref[column, :, 0:size], rows_dev, head_dim, offset, width)
+        key_grad = gather_heads(total_ref[column], rows_dev, head_dim) * scaling
+        value_grad = gather_heads(
+            value_total_ref[column, :, 0:size], rows_dev, head_dim, offset, width
         )
+        key_grads.append(jnp.where(own_open, key_grad, 0.0))
+        value_grads.append(jnp.where(own_open, value_grad, 0.0))
     item_grads = [
         jnp.concatenate(parts, axis=0).astype(BF16)
         for parts in (query_grads, key_grads, value_grads)
@@ -1193,28 +1324,33 @@
     swap = swap_copy(branch_ref, peer_branch_ref, swap_sem.at[2], swap_sem.at[3])
     swap.start()
 
-    def side_by_side(left, right):
-        return jnp.concatenate([left, right], axis=1).astype(BF16)
-
-    early_ref[0:width, :] = side_by_side(
-        dot_tn(first_low, item_grads[0]), dot_tn(first_low, item_grads[1])
-    )
-    early_ref[width : 2 * width, :] = side_by_side(
-        dot_tn(first_low, item_grads[2]), item_out_grad
-    )
-    if early_ref.shape[0] > 4 * width:
-        early_ref[4 * width :, :] = jnp.zeros((early_ref.shape[0] - 4 * width, 2 * width), BF16)
-    early_sum.scatter_start(0)
-    banks_gather.across_side(0)
-    for k in range(1, rows_count // 4):
-        banks_gather.along_depth(k)
-    early_sum.scatter_finish(0)
-    early_sum.scatter_start(1)
-    for k in range(1, rows_count // 4):
-        banks_gather.across_side(k)
-
     own_branch = first_in_grad.astype(BF16)
-    feat_out_grad = dot_tn(feat_mixed, own_branch)
+    row = put_tiles(
+        item_part_ref,
+        0,
+        jnp.concatenate([dot_tn(first_low, item_grads[n]) for n in range(2)], axis=1),
+    )
+    row = put_tiles(
+        item_part_ref,
+        row,
+        jnp.concatenate(
+            [dot_tn(first_low, item_grads[2]), dot_tn(feat_mixed, own_branch)], axis=1
+        ),
+    )
+    pairs = [
+        jnp.concatenate(pair, axis=1)
+        for pair in ((gain_one, shift_one), (gain_two, shift_two), (gain_three, shift_three))
+    ]
+    row = put_tiles(
+        item_part_ref, row, jnp.concatenate(pairs + [jnp.zeros((13, 2 * width), F32)], axis=0)
+    )
+    put_zeros(item_part_ref, row)
+    item_sum.scatter_start(0)
+    mlp_sum.scatter_finish(2)
+    mlp_sum.gather_start(2)
+    item_sum.scatter_finish(0)
+    item_sum.scatter_start(1)
+
     swap.wait()
     peer_branch = stack_columns(peer_branch_ref[...].astype(F32), width).astype(BF16)
     all_branch = jnp.concatenate([own_branch, peer_branch], axis=0)
@@ -1227,8 +1363,10 @@
     score_grads = [
         (weight * (dot - row_delta)).astype(BF16) for weight, dot in zip(weights, dots)
     ]
-    early_sum.scatter_finish(1)
-    early_sum.scatter_start(2)
+    mlp_sum.gather_finish(2)
+    mlp_sum.gather_start(1)
+    item_sum.scatter_finish(1)
+    item_sum.scatter_start(2)
     query_grad = None
     for score_grad, part in zip(score_grads, key_list):
         added = dot_nn(score_grad[:own_count], wide) * tile_rows(part, cols_dev)
@@ -1249,34 +1387,30 @@
         (jnp.concatenate(key_parts, axis=0) * scaling).astype(BF16),
         jnp.concatenate(value_parts, axis=0).astype(BF16),
     ]
-    late_ref[0:width, :] = side_by_side(
-        dot_tn(own_low, feat_grads[0]), dot_tn(own_low, feat_grads[1])
-    )
-    late_ref[width : 2 * width, :] = side_by_side(dot_tn(own_low, feat_grads[2]), feat_out_grad)
-    pairs = [
-        jnp.concatenate(pair, axis=1)
-        for pair in ((gain_one, shift_one), (gain_two, shift_two), (gain_three, shift_three))
-    ]
-    rest = late_ref.shape[0] - 2 * width - len(pairs)
-    late_ref[2 * width :, :] = jnp.concatenate(
-        pairs + [jnp.zeros((rest, 2 * width), F32)], axis=0
-    ).astype(BF16)
-    late_sum.scatter_start(0)
-    early_sum.scatter_finish(2)
-    early_sum.gather_start(2)
-    late_sum.scatter_finish(0)
-    late_sum.scatter_start(1)
+    row = put_tiles(
+        feat_part_ref,
+        0,
+        jnp.concatenate([dot_tn(own_low, feat_grads[n]) for n in range(2)], axis=1),
+    )
+    row = put_tiles(feat_part_ref, row, dot_tn(own_low, feat_grads[2]))
+    put_zeros(feat_part_ref, row)
+    feat_sum.scatter_start(0)
+    item_sum.scatter_finish(2)
+    item_sum.gather_start(2)
+    feat_sum.scatter_finish(0)
+    feat_sum.scatter_start(1)
     inner = None
     for n in range(3):
         added = dot_nt(feat_grads[n], feat_w[n])
         inner = added if inner is None else inner + added
     cells_grad_ref[...] = pack_columns(first_in_grad + inner.astype(BF16).astype(F32), rows_dev)
+    results.append(mover.start(cells_grad_ref, cells_grad_out))
     for k in range(rows_count // 4):
         banks_gather.from_core(k, 0)
         banks_gather.from_core(k, 1)
     sort_rows = sorted_ref.shape[0]
     sort_block = math.gcd(sort_rows, 256)
-    owner = owner_ref[...]
+    owner = owner_ref[...].reshape(1, sort_rows)
 
     def sort_some(first, last):
         @pl.loop(first, last)
@@ -1287,25 +1421,31 @@
             sorted_ref[pl.ds(start, sort_block), :] = dot_nn(chosen, banks_ref[...]).astype(BF16)
 
     thirds = sort_rows // sort_block // 3
-    early_sum.gather_finish(2)
-    early_sum.gather_start(1)
-    late_sum.scatter_finish(1)
-    late_sum.scatter_start(2)
+    mlp_sum.gather_finish(1)
+    mlp_sum.gather_start(0)
+    item_sum.gather_finish(2)
+    item_sum.gather_start(1)
+    feat_sum.scatter_finish(1)
+    feat_sum.scatter_start(2)
     sort_some(0, thirds)
-    early_sum.gather_finish(1)
-    early_sum.gather_start(0)
-    late_sum.scatter_finish(2)
-    late_sum.gather_start(2)
+    item_sum.gather_finish(1)
+    item_sum.gather_start(0)
+    feat_sum.scatter_finish(2)
+    feat_sum.gather_start(2)
     sort_some(thirds, 2 * thirds)
-    late_sum.gather_finish(2)
-    late_sum.gather_start(1)
-    early_sum.gather_finish(0)
+    feat_sum.gather_finish(2)
+    feat_sum.gather_start(1)
     sort_some(2 * thirds, sort_rows // sort_block)
-    late_sum.gather_finish(1)
-    late_sum.gather_start(0)
+    results.append(mover.start(sorted_ref, sorted_out))
+    mlp_sum.gather_finish(0)
+    item_sum.gather_finish(0)
+    feat_sum.gather_finish(1)
+    feat_sum.gather_start(0)
     for gather in (hidden_gather, grads_gather, banks_gather):
         gather.wait_sent()
-    late_sum.gather_finish(0)
+    for result in results:
+        result.wait()
+    feat_sum.gather_finish(0)
 
 
 def moment_rule(gradient, first_old, second_old):
@@ -1324,88 +1464,165 @@
 
 def update_kernel(
     owner_ref,
-    layer_ref,
-    cells_grad_ref,
-    early_ref,
-    late_ref,
-    sorted_ref,
-    small_ref,
-    big_ref,
-    first_ref,
-    second_ref,
-    proj_ref,
-    feat_out_ref,
-    item_out_ref,
-    mlp_in_ref,
-    mlp_out_ref,
+    mlp_sum_ref,
+    item_sum_ref,
+    feat_sum_ref,
     gains_ref,
     shifts_ref,
     norm_first_ref,
     norm_second_ref,
-    layer_out_ref,
-    cells_out_ref,
-    square_grad_ref,
-    in_grad_ref,
-    out_grad_ref,
+    first_ref,
+    second_ref,
+    small_in,
+    big_in,
+    sorted_in,
+    proj_in,
+    feat_out_in,
+    item_out_in,
+    mlp_in_in,
+    mlp_out_in,
+    layer_in,
+    cells_grad_in,
+    layer_out,
+    cells_grad_out,
+    square_grad_out,
+    in_grad_out,
+    out_grad_out,
     norm_grad_ref,
     clip_ref,
     first_new_ref,
     second_new_ref,
+    square_new_out,
+    in_new_out,
+    out_new_out,
+    square_low_out,
+    in_low_out,
+    out_low_out,
+    norm_new_ref,
+    norm_first_new_ref,
+    norm_second_new_ref,
+    small_ref,
+    big_ref,
+    sorted_ref,
+    olds_ref,
+    mlp_in_ref,
+    mlp_out_ref,
+    square_grad_ref,
+    in_grad_ref,
+    out_grad_ref,
     square_new_ref,
     in_new_ref,
     out_new_ref,
     square_low_ref,
     in_low_ref,
     out_low_ref,
-    norm_new_ref,
-    norm_first_new_ref,
-    norm_second_new_ref,
     rotated_ref,
     own_ref,
+    move_sem,
 ):
     width, ff_width = mlp_in_ref.shape
     slots = first_ref.shape[0]
-    layer_out_ref[...] = layer_ref[...]
-    cells_out_ref[...] = cells_grad_ref[...]
-
-    early = early_ref[...].astype(F32)
-    late = late_ref[...].astype(F32)
+    squares = square_grad_ref.shape[0]
+    mover = Mover(move_sem)
+    small_loads = [
+        (
+            mover.start(small_in.at[n], small_ref.at[n]),
+            mover.start(small_in.at[squares + n], small_ref.at[squares + n]),
+        )
+        for n in range(squares)
+    ]
+    last_loads = [
+        mover.start(small_in.at[2 * squares], small_ref.at[2 * squares]),
+        mover.start(small_in.at[2 * squares + 1], small_ref.at[2 * squares + 1]),
+        mover.start(big_in, big_ref),
+    ]
+    sorted_load = mover.start(sorted_in, sorted_ref)
+    old_loads = [
+        mover.start(proj_in, olds_ref.at[0 : squares - 2]),
+        mover.start(feat_out_in, olds_ref.at[squares - 2]),
+        mover.start(item_out_in, olds_ref.at[squares - 1]),
+    ]
+    mlp_loads = [mover.start(mlp_in_in, mlp_in_ref), mover.start(mlp_out_in, mlp_out_ref)]
+    results = [mover.start(layer_in, layer_out), mover.start(cells_grad_in, cells_grad_out)]
+
     square = None
-    for part in (early, late):
+    for part_ref in (mlp_sum_ref, item_sum_ref, feat_sum_ref):
+        part = part_ref[...].astype(F32)
         added = jnp.sum(jnp.sum(part * part, axis=1, keepdims=True), axis=0, keepdims=True)
         square = added if square is None else square + added
     grad_norm = jnp.sqrt(square)
     factor = jnp.minimum(1.0, CLIP_NORM / grad_norm)
     clip_ref[0] = grad_norm[0, 0]
-    early = early * factor
-    late = late * factor
-    squares = [
-        part[row : row + width, lane : lane + width]
-        for part, row, lane in (
-            (late, 0, 0),
-            (late, 0, width),
-            (late, width, 0),
-            (early, 0, 0),
-            (early, 0, width),
-            (early, width, 0),
-            (late, width, width),
-            (early, width, width),
-        )
+    both_width = 2 * width
+    both_tiles = both_width // LANES * width
+    feat_pair = take_tiles(feat_sum_ref, 0, width, both_width) * factor
+    item_pair = take_tiles(item_sum_ref, 0, width, both_width) * factor
+    mixed_pair = take_tiles(item_sum_ref, both_tiles, width, both_width) * factor
+    parts = [
+        feat_pair[:, :width],
+        feat_pair[:, width:],
+        take_tiles(feat_sum_ref, both_tiles, width, width) * factor,
+        item_pair[:, :width],
+        item_pair[:, width:],
+        mixed_pair[:, :width],
+        mixed_pair[:, width:],
+        take_tiles(mlp_sum_ref, 2 * both_tiles, width, width) * factor,
     ]
-    for n, clipped in enumerate(squares):
+    for n, clipped in enumerate(parts):
         square_grad_ref[n] = clipped
-        turned = dot_fine(dot_nn, clipped, small_ref[8 + n])
-        rotated_ref[n * width : (n + 1) * width, :] = dot_fine(dot_tn, small_ref[n], turned)
-    start = len(squares) * width
+        for load in small_loads[n]:
+            load.wait()
+        turned = dot_low(dot_nn, clipped, small_ref[squares + n])
+        rotated_ref[n * width : (n + 1) * width, :] = dot_low(dot_tn, small_ref[n], turned)
+    results.append(mover.start(square_grad_ref, square_grad_out))
+    start = squares * width
     middle = start + ff_width
-    clipped = early[2 * width : 3 * width]
+    for load in last_loads:
+        load.wait()
+    clipped = take_tiles(mlp_sum_ref, 0, width, ff_width) * factor
     in_grad_ref[...] = clipped
-    turned = dot_fine(dot_tn, clipped, small_ref[16])
-    rotated_ref[start:middle, :] = dot_fine(dot_tn, big_ref[0], turned)
-    clipped = early[3 * width : 4 * width]
+    results.append(mover.start(in_grad_ref, in_grad_out))
+    turned = dot_low(dot_tn, clipped, small_ref[2 * squares])
+    rotated_ref[start:middle, :] = dot_low(dot_tn, big_ref[0], turned)
+    clipped = take_tiles(mlp_sum_ref, both_tiles, width, ff_width) * factor
     out_grad_ref[...] = clipped
-    turned = dot_fine(dot_tn, clipped, small_ref[17])
-    rotated_ref[middle : middle + ff_width, :] = dot_fine(dot_tn, big_ref[1], turned)
+    results.append(mover.start(out_grad_ref, out_grad_out))
+    turned = dot_low(dot_tn, clipped, small_ref[2 * squares + 1])
+    rotated_ref[middle : middle + ff_width, :] = dot_low(dot_tn, big_ref[1], turned)
+
+    def step_of(first_row, count):
+        rows = slice(first_row, first_row + count)
+        banks = sorted_ref[rows, :].astype(F32)
+        return moment_rule(rotated_ref[rows, :], banks[:, :width], banks[:, width:])[2]
+
+    sorted_load.wait()
+    for load in old_loads:
+        load.wait()
+    for n in range(squares):
+        turned = dot_low(dot_nt, step_of(n * width, width), small_ref[squares + n])
+        update = dot_low(dot_nn, small_ref[n], turned)
+        old = olds_ref[n]
+        new = old - LEARN_RATE * root_mean(old) * update
+        square_new_ref[n] = new
+        square_low_ref[n] = new.astype(BF16)
+        results.append(mover.start(square_new_ref.at[n], square_new_out.at[n]))
+    results.append(mover.start(square_low_ref, square_low_out))
+    for load in mlp_loads:
+        load.wait()
+    turned = dot_low(dot_nn, big_ref[0], step_of(start, ff_width))
+    update = dot_low(dot_nt, small_ref[2 * squares], turned)
+    new = mlp_in_ref[...] - LEARN_RATE * root_mean(mlp_in_ref[...]) * update
+    in_new_ref[...] = new
+    in_low_ref[...] = new.astype(BF16)
+    results.append(mover.start(in_new_ref, in_new_out))
+    results.append(mover.start(in_low_ref, in_low_out))
+    turned = dot_low(dot_nn, big_ref[1], step_of(middle, ff_width))
+    update = dot_low(dot_nt, small_ref[2 * squares + 1], turned)
+    new = mlp_out_ref[...] - LEARN_RATE * root_mean(mlp_out_ref[...]) * update
+    out_new_ref[...] = new
+    out_low_ref[...] = new.astype(BF16)
+    results.append(mover.start(out_new_ref, out_new_out))
+    results.append(mover.start(out_low_ref, out_low_out))
 
     base = lax.axis_index("rows") * slots
 
@@ -1419,31 +1636,9 @@
     first_new_ref[...] = first_new
     second_new_ref[...] = second_new
 
-    def step_of(first_row, count):
-        rows = slice(first_row, first_row + count)
-        banks = sorted_ref[rows, :].astype(F32)
-        return moment_rule(rotated_ref[rows, :], banks[:, :width], banks[:, width:])[2]
-
-    for n in range(len(squares)):
-        turned = dot_fine(dot_nt, step_of(n * width, width), small_ref[8 + n])
-        update = dot_fine(dot_nn, small_ref[n], turned)
-        old = proj_ref[n] if n < 6 else (feat_out_ref if n == 6 else item_out_ref)[...]
-        new = old - LEARN_RATE * root_mean(old) * update
-        square_new_ref[n] = new
-        square_low_ref[n] = new.astype(BF16)
-    turned = dot_fine(dot_nn, big_ref[0], step_of(start, ff_width))
-    update = dot_fine(dot_nt, small_ref[16], turned)
-    new = mlp_in_ref[...] - LEARN_RATE * root_mean(mlp_in_ref[...]) * update
-    in_new_ref[...] = new
-    in_low_ref[...] = new.astype(BF16)
-    turned = dot_fine(dot_nn, big_ref[1], step_of(middle, ff_width))
-    update = dot_fine(dot_nt, small_ref[17], turned)
-    new = mlp_out_ref[...] - LEARN_RATE * root_mean(mlp_out_ref[...]) * update
-    out_new_ref[...] = new
-    out_low_ref[...] = new.astype(BF16)
-
+    norm_pairs = take_tiles(item_sum_ref, 2 * both_tiles, 16, both_width) * factor
     for n in range(3):
-        pair = late[2 * width + n : 2 * width + n + 1]
+        pair = norm_pairs[n : n + 1]
         both = jnp.concatenate([pair[:, :width], pair[:, width:]], axis=0)
         norm_grad_ref[n] = both
         first_new, second_new, change = moment_rule(both, norm_first_ref[n], norm_second_ref[n])
@@ -1452,10 +1647,16 @@
         old = jnp.concatenate([gains_ref[n : n + 1, :], shifts_ref[n : n + 1, :]], axis=0)
         size = jnp.sqrt(jnp.sum(old * old, axis=1, keepdims=True) * (1.0 / width) + 1e-06)
         norm_new_ref[n] = old - LEARN_RATE * size * change
+    for result in results:
+        result.wait()
 
 
 def in_vmem():
     return pl.BlockSpec(memory_space=pltpu.VMEM)
+
+
+def anywhere():
+    return pl.BlockSpec(memory_space=pl.ANY)
 
 
 def in_smem():
@@ -1485,6 +1686,7 @@
     rows_count, cols_count = lax.axis_size("rows"), lax.axis_size("cols")
     rows_dev, width_dev = cells.shape
     width = proj_weights.shape[-1]
+    ff_width = mlp_in.shape[1]
     cols_dev = width_dev // width
     rows_all = rows_dev * rows_count
     key_total = rows_all // 4 * 3
@@ -1509,28 +1711,44 @@
         for stage in STAGES:
             count = members(stage, sizes)
             rows //= count
-            found.append(pltpu.VMEM((count - 1, rows, 2 * width), BF16))
+            found.append(pltpu.VMEM((count - 1, rows, LANES), BF16))
         return found
 
-    early_rows = block_rows(4 * width)
-    late_rows = block_rows(2 * width + 3)
+    both_tiles = 2 * width // LANES * width
+    half_tiles = -(-width // LANES) * width
+    sum_rows = [
+        block_rows(2 * (ff_width // LANES) * width + half_tiles),
+        block_rows(2 * both_tiles + 2 * width // LANES * 16),
+        block_rows(both_tiles + half_tiles),
+    ]
     widest = max(members(stage, sizes) for stage in STAGES) - 1
-    layer_part, cells_part, early_total, late_total, sorted_banks = pl.pallas_call(
+    layer_part, cells_part, mlp_total, item_total, feat_total, sorted_banks = pl.pallas_call(
         functools.partial(layer_kernel, rows_count, cols_count),
         name="layer_and_gradients",
         out_shape=(
             shape((rows_dev, width_dev), BF16),
             shape((rows_dev, width_dev), F32),
-            shape((early_rows, 2 * width), BF16),
-            shape((late_rows, 2 * width), BF16),
+            *[shape((rows, LANES), BF16) for rows in sum_rows],
             shape((bank_rows, 2 * width), BF16),
         ),
-        in_specs=[in_smem()] + [in_vmem()] * 13,
-        out_specs=[in_vmem()] * 5,
+        in_specs=[in_smem()] + [in_vmem()] * 5 + [anywhere()] * 8,
+        out_specs=[anywhere()] * 2 + [in_vmem()] * 3 + [anywhere()],
         scratch_shapes=[
+            pltpu.VMEM(proj_weights.shape, F32),
+            pltpu.VMEM(feat_out_w.shape, F32),
+            pltpu.VMEM(bank_first.shape, F32),
+            pltpu.VMEM(bank_first.shape, F32),
+            pltpu.VMEM(item_out_w.shape, F32),
+            pltpu.VMEM(mlp_in.shape, F32),
+            pltpu.VMEM(mlp_in.shape, F32),
+            pltpu.VMEM((rows_dev, width_dev), BF16),
+            pltpu.VMEM((rows_dev, width_dev), BF16),
+            pltpu.VMEM((rows_dev, width_dev), F32),
+            pltpu.VMEM((bank_rows, 2 * width), BF16),
             pltpu.VMEM((rows_dev, width_dev), BF16),
             pltpu.VMEM((rows_all, width_dev), BF16),
             pltpu.VMEM((cols_dev, key_total, width), BF16),
+            pltpu.VMEM((cols_dev, width, key_total), BF16),
             pltpu.VMEM((cols_dev, key_total, width), BF16),
             pltpu.VMEM((rows_all, width_dev), BF16),
             pltpu.VMEM((16 * cols_dev, rows_all), F32),
@@ -1538,44 +1756,44 @@
             pltpu.VMEM((cols_dev, head_rows, width), BF16),
             pltpu.VMEM((cols_dev, head_rows, width), BF16),
             pltpu.VMEM((cols_dev, head_rows, 2 * LANES), BF16),
-            pltpu.VMEM((cols_dev, head_rows, 1), F32),
-            pltpu.VMEM((cols_dev, head_rows, 1), F32),
+            pltpu.VMEM((cols_dev, 1, head_rows), F32),
+            pltpu.VMEM((cols_dev, 1, head_rows), F32),
+            pltpu.VMEM((cols_dev, width, head_rows), F32),
             pltpu.VMEM((cols_dev, head_rows, width), F32),
             pltpu.VMEM((cols_dev, head_rows, 2 * LANES), F32),
             pltpu.VMEM((cols_dev, 3, 2 * LANES, width), BF16),
+            pltpu.VMEM((cols_dev, 2, width, 2 * LANES), BF16),
             pltpu.VMEM((rows_dev, width_dev), BF16),
             pltpu.VMEM((rows_dev, width_dev), BF16),
-            pltpu.VMEM((early_rows, 2 * width), BF16),
-            pltpu.VMEM((late_rows, 2 * width), BF16),
         ]
-        + landings(early_rows)
-        + landings(late_rows)
+        + [pltpu.VMEM((rows, LANES), BF16) for rows in sum_rows]
+        + [landing for rows in sum_rows for landing in landings(rows)]
         + [
             dma((4,)),
             dma((2, 1, slots)),
             dma((2, 2, slots)),
             dma((2, 1, slots)),
-            dma((4, len(STAGES), widest)),
-            dma((4, len(STAGES), widest)),
-        ],
+        ]
+        + [dma((4, len(STAGES), widest))] * len(sum_rows)
+        + [dma((11,))],
         compiler_params=pltpu.CompilerParams(
             collective_id=0, has_side_effects=True, vmem_limit_bytes=VMEM_BYTES
         ),
     )(
         train_rows,
-        owner_rows.reshape(1, bank_rows),
+        owner_rows,
         cells,
         mask_rows,
-        cotangent,
+        norm_gains,
+        norm_shifts,
         proj_weights,
         feat_out_w,
+        bank_first,
+        bank_second,
         item_out_w,
         mlp_in,
         mlp_out_turned,
-        norm_gains,
-        norm_shifts,
-        bank_first,
-        bank_second,
+        cotangent,
     )
 
     slots_dev = bank_first.shape[0]
@@ -1622,33 +1840,53 @@
             shape(norm_first_turned.shape, F32),
             shape(norm_first_turned.shape, F32),
         ),
-        in_specs=[in_smem()] + [in_vmem()] * 18,
-        out_specs=[in_vmem()] * 6 + [in_smem()] + [in_vmem()] * 11,
+        in_specs=[in_smem()] + [in_vmem()] * 9 + [anywhere()] * 10,
+        out_specs=[anywhere()] * 5
+        + [in_vmem(), in_smem(), in_vmem(), in_vmem()]
+        + [anywhere()] * 6
+        + [in_vmem()] * 3,
         scratch_shapes=[
+            pltpu.VMEM(bases_small.shape, F32),
+            pltpu.VMEM(bases_big.shape, F32),
+            pltpu.VMEM(sorted_banks.shape, BF16),
+            pltpu.VMEM(square, F32),
+            pltpu.VMEM(mlp_in.shape, F32),
+            pltpu.VMEM(mlp_in.shape, F32),
+            pltpu.VMEM(square, F32),
+            pltpu.VMEM(mlp_in.shape, F32),
+            pltpu.VMEM(mlp_in.shape, F32),
+            pltpu.VMEM(square, F32),
+            pltpu.VMEM(mlp_in.shape, F32),
+            pltpu.VMEM(mlp_in.shape, F32),
+            pltpu.VMEM(square, BF16),
+            pltpu.VMEM(mlp_in.shape, BF16),
+            pltpu.VMEM(mlp_in.shape, BF16),
             pltpu.VMEM((bank_rows, width), F32),
             pltpu.VMEM((slots_dev, width), F32),
+            dma((48,)),
         ],
         compiler_params=pltpu.CompilerParams(vmem_limit_bytes=VMEM_BYTES),
     )(
         owner_rows,
-        layer_part,
-        cells_part,
-        early_total,
-        late_total,
-        sorted_banks,
+        mlp_total,
+        item_total,
+        feat_total,
+        norm_gains,
+        norm_shifts,
+        norm_first_turned,
+        norm_second_turned,
+        bank_first,
+        bank_second,
         bases_small,
         bases_big,
-        bank_first,
-        bank_second,
+        sorted_banks,
         proj_weights,
         feat_out_w,
         item_out_w,
         mlp_in,
         mlp_out_turned,
-        norm_gains,
-        norm_shifts,
-        norm_first_turned,
-        norm_second_turned,
+        layer_part,
+        cells_part,
     )
     return (
         layer_out,

time: 133 us -> 114 us (0.86)
  Pallas kernels: 130 us -> 112 us
    pallas_call x1, Pallas kernels: 116 us -> 99.3 us  [fast_device(): pl.pallas_call(functools.partial(layer_kernel, rows_count, cols_count), n...]
where the time goes in v1:
time: 114 us; the launch traced here: 113 us
  Pallas kernels  112 us (98%)
  between operations  1.49 us (1%)
    pallas_call x1, Pallas kernels, fast_device(): pl.pallas_call(functools.partial(layer_kernel, rows_count, cols_count), n...  99.3 us
    pallas_call x1, Pallas kernels, fast_device(): pl.pallas_call(update_kernel, name='rotated_update', out_shape=(shape(lay...  12.7 us

profile of v1, /device:TPU:0, one launch (start us, length us, event | category | flops | bytes accessed | tf_op | source)
XLA Modules:
  0.0 113.5 jit_solution(12123863326239402722)
XLA Ops:
  1.3 99.3 %layer_and_gradients.1 = (bf16[128,384]{1,0:T(8,128)(2,1)}, f32[128,384]{1,0:T(8,128)}, bf16[1536,128]{1,0:T(8,128)(2,1)}, bf16[1536,128]{1,0:T(8,128)(2,1)}, bf...) custom-call(s32[1]{0:T(128)S(6)} %copy.36.train_ref, s32[2304]{0:T(1024)} %owner_ref.3, bf16[128,384]{1,0:T(8,128)(2,1)} %cells_ref.1, ...), custom_call_target="tpu_custom_call" | custom-call | tf_op jit(solution)/shard_map/layer_and_gradients/pallas_call | solution.py:1725
  100.6 12.7 %rotated_update.1 = (bf16[128,384]{1,0:T(8,128)(2,1)}, f32[128,384]{1,0:T(8,128)}, f32[8,192,192]{2,1,0:T(8,128)}, f32[192,384]{1,0:T(8,128)}, f32[192,384]{1,0:...) custom-call(s32[2304]{0:T(1024)} %owner_ref.3, ...), custom_call_target="tpu_custom_call" | custom-call | tf_op jit(solution)/shard_map/rotated_update/pallas_call | solution.py:1820

commit v2 on v1

--- a/solution.py
+++ b/solution.py
@@ -563,24 +563,13 @@
     return dot_nn(high, table) + dot_nn(low, table)
 
 
-def head_mask(rows, width, head_dim, head, offset=0):
+def head_mask(rows, width, head_dim, head):
     feature = lax.broadcasted_iota(jnp.int32, (rows, width), 1)
-    start = offset + head * head_dim
-    return (feature >= start) & (feature < start + head_dim)
+    return (feature >= head * head_dim) & (feature < (head + 1) * head_dim)
 
 
 def tile_rows(value, count):
     return jnp.concatenate([value] * count, axis=0)
-
-
-def column_open(mask_ref, own_first, cols_dev, slot):
-    table = jnp.transpose(mask_ref[...].astype(F32))
-    if slot < cols_dev:
-        first, second = slot, slot + cols_dev
-    else:
-        first, second = slot, slot - cols_dev
-    picked = jnp.where(own_first, table[:, first : first + 1], table[:, second : second + 1])
-    return picked > 0.0
 
 
 def feature_weights(queries, key_list, open_list, repeat, table, scaling):
@@ -676,20 +665,28 @@
         shard = self.place(self.source(k), side, 1 - self.core)
         self.arrive(shard, self.core_peer(), (2 + other_side) * self.deep - 1 + k)
 
-    def run(self, use):
-        self.across_side(0)
-
+    def forward(self, k):
+        self.across_side(k)
+
+        @pl.when(k + 1 < self.deep)
+        def _():
+            self.along_depth(k + 1)
+
+    def run(self, use, forwarded):
         @pl.loop(0, 2 * self.deep)
         def _(turn):
             k, other = turn // 2, turn % 2
-
-            @pl.when((k + 1 < self.deep) & (other == 0))
-            def _():
-                self.along_depth(k + 1)
-
-            @pl.when((k + 1 < self.deep) & (other == 1))
-            def _():
-                self.across_side(k + 1)
+            if forwarded:
+
+                @pl.when((other == 0) & (k > 0) & (k + forwarded - 1 < self.deep))
+                def _():
+                    self.forward(k + forwarded - 1)
+
+            else:
+
+                @pl.when((turn == 1) | ((other == 0) & (k > 0)))
+                def _():
+                    self.forward(k)
 
             self.from_core(k, other)
             use(self.source(k), self.side + other - 2 * self.side * other)
@@ -701,6 +698,142 @@
         def _(slot):
             for copy in self.copies(own, self.core_peer(), slot):
                 copy.wait_send()
+
+
+class DepthGather:
+    def __init__(self, pieces, send_sem, recv_sem, rows_count):
+        self.pieces, self.send_sem, self.recv_sem = pieces, send_sem, recv_sem
+        self.deep = rows_count // 4
+        me = lax.axis_index("rows")
+        self.core, self.side, self.depth = me % 2, (me // 2) % 2, me // 4
+
+    @staticmethod
+    def slots(rows_count):
+        return rows_count // 2 - 1
+
+    def row(self, depth, core):
+        return (depth * 2 + self.side) * 2 + core
+
+    def source(self, k):
+        return flip(self.depth, k, self.deep)
+
+    def copies(self, shard, target, slot):
+        return [
+            pltpu.make_async_remote_copy(
+                src_ref=piece(shard),
+                dst_ref=piece(shard),
+                send_sem=self.send_sem.at[n, slot],
+                recv_sem=self.recv_sem.at[n, slot],
+                device_id={"rows": target},
+                device_id_type=MESH,
+            )
+            for n, piece in enumerate(self.pieces)
+        ]
+
+    def start(self):
+        own = self.depth * 2 + self.core
+        for copy in self.copies(own, self.row(self.depth, 1 - self.core), self.deep - 1):
+            copy.start()
+        for k in range(1, self.deep):
+            for copy in self.copies(own, self.row(self.source(k), self.core), k - 1):
+                copy.start()
+
+    def forward(self, k):
+        shard = self.source(k) * 2 + self.core
+        for copy in self.copies(shard, self.row(self.source(k), self.core), k - 1):
+            copy.wait_recv()
+        twin = self.row(self.depth, 1 - self.core)
+        for copy in self.copies(shard, twin, self.deep - 1 + k):
+            copy.start()
+
+    def run(self, use, forwarded):
+        twin = self.row(self.depth, 1 - self.core)
+
+        @pl.loop(0, 2 * self.deep)
+        def _(turn):
+            k, other = turn // 2, turn % 2
+
+            @pl.when((other == 0) & (k > forwarded))
+            def _():
+                self.forward(k)
+
+            @pl.when(other == 1)
+            def _():
+                shard = self.source(k) * 2 + 1 - self.core
+                for copy in self.copies(shard, twin, self.deep - 1 + k):
+                    copy.wait_recv()
+
+            use(self.source(k), self.core + other - 2 * self.core * other)
+
+    def wait_sent(self):
+        own = self.depth * 2 + self.core
+
+        @pl.loop(0, 2 * self.deep - 1)
+        def _(slot):
+            for copy in self.copies(own, self.row(self.depth, 1 - self.core), slot):
+                copy.wait_send()
+
+
+class Quad:
+    def __init__(self):
+        row = lax.axis_index("rows")
+        self.side, self.col = (row // 2) % 2, lax.axis_index("cols")
+        self.row = row
+        self.own = self.side * 2 + self.col
+
+    def device(self, pattern):
+        side_flip, col_flip = pattern % 2, pattern // 2
+        side = self.side + side_flip - 2 * self.side * side_flip
+        col = self.col + col_flip - 2 * self.col * col_flip
+        return {"rows": self.row + 2 * (side - self.side), "cols": col}
+
+    def number(self, pattern):
+        side_flip, col_flip = pattern % 2, pattern // 2
+        side = self.side + side_flip - 2 * self.side * side_flip
+        return side * 2 + self.col + col_flip - 2 * self.col * col_flip
+
+    def spread(self, source, landing, sem):
+        return [
+            pltpu.make_async_remote_copy(
+                src_ref=source,
+                dst_ref=landing.at[self.own],
+                send_sem=sem.at[0, pattern - 1],
+                recv_sem=sem.at[1, pattern - 1],
+                device_id=self.device(pattern),
+                device_id_type=MESH,
+            )
+            for pattern in range(1, 4)
+        ]
+
+    def across(self, source, landing, sem):
+        return pltpu.make_async_remote_copy(
+            src_ref=source,
+            dst_ref=landing,
+            send_sem=sem.at[0],
+            recv_sem=sem.at[1],
+            device_id=self.device(1),
+            device_id_type=MESH,
+        )
+
+    def pick(self, packed, width, other):
+        left, right = packed[:, :width], packed[:, width:]
+        return jnp.where(self.side == other, left, right)
+
+    def joined(self, own, other):
+        return jnp.concatenate(
+            [jnp.where(self.side == 0, own, other), jnp.where(self.side == 0, other, own)], axis=1
+        )
+
+    def columns(self, landing, width):
+        found = []
+        for col_flip in range(2):
+            col = self.col + col_flip - 2 * self.col * col_flip
+            blocks = [landing[side * 2 + col].astype(F32) for side in range(2)]
+            for other in range(2):
+                found.append(
+                    jnp.concatenate([self.pick(block, width, other) for block in blocks], axis=0)
+                )
+        return found
 
 
 class StagedSum:
@@ -710,7 +843,7 @@
         row = lax.axis_index("rows")
         self.me = {"z": row // 4, "x": (row // 2) % 2, "k": row % 2, "y": lax.axis_index("cols")}
         self.spans, base, size = [], 0, part_ref.shape[0]
-        for stage in stages:
+        for stage in stages[:-1]:
             size = size // members(stage, sizes)
             self.spans.append((base, size))
             base = base + self.number(self.me, stage) * size
@@ -769,8 +902,43 @@
             total = total + self.landing[s][j].astype(F32)
         for copy in copies:
             copy.wait_send()
-        target = self.total_ref if s == len(self.stages) - 1 else self.part_ref
-        target[rows, :] = total.astype(BF16)
+        self.part_ref[rows, :] = total.astype(BF16)
+
+    def share(self):
+        last = len(self.stages) - 1
+        stage, landing = self.stages[last], self.landing[last]
+        rows = self.rows_at(self.base, self.size)
+        own = self.number(self.me, stage)
+        found = []
+        for j in range(1, members(stage, self.sizes)):
+            found.append(
+                pltpu.make_async_remote_copy(
+                    src_ref=self.part_ref.at[rows, :],
+                    dst_ref=landing.at[own],
+                    send_sem=self.sems.at[0, last, j - 1],
+                    recv_sem=self.sems.at[1, last, j - 1],
+                    device_id=self.device(self.partner(stage, j)),
+                    device_id_type=MESH,
+                )
+            )
+        return found
+
+    def share_start(self):
+        for copy in self.share():
+            copy.start()
+        own = self.number(self.me, self.stages[-1])
+        self.landing[-1][own] = self.part_ref[self.rows_at(self.base, self.size), :]
+
+    def share_finish(self):
+        copies = self.share()
+        for copy in copies:
+            copy.wait_recv()
+        total = self.landing[-1][0].astype(F32)
+        for n in range(1, members(self.stages[-1], self.sizes)):
+            total = total + self.landing[-1][n].astype(F32)
+        for copy in copies:
+            copy.wait_send()
+        self.total_ref[self.rows_at(self.base, self.size), :] = total.astype(BF16)
 
     def gather(self, s, own):
         stage, (base, size) = self.stages[s], self.spans[s]
@@ -846,59 +1014,10 @@
     pl.semaphore_wait(barrier, len(targets))
 
 
-def swap_copy(source, landing, send_sem, recv_sem):
-    return pltpu.make_async_remote_copy(
-        src_ref=source,
-        dst_ref=landing,
-        send_sem=send_sem,
-        recv_sem=recv_sem,
-        device_id={"cols": 1 - lax.axis_index("cols")},
-        device_id_type=MESH,
-    )
-
-
-def window_of(column, width, width_dev):
-    start = (column * width) // LANES * LANES
-    offset = column * width - start
-    size = -(-(offset + width) // LANES) * LANES
-    return start, offset, min(size, width_dev - start)
-
-
-def padded_weight(weight, offset, size):
-    width = weight.shape[1]
-    parts = []
-    if offset:
-        parts.append(jnp.zeros((offset, width), F32))
-    parts.append(weight)
-    if size - offset - weight.shape[0]:
-        parts.append(jnp.zeros((size - offset - weight.shape[0], width), F32))
-    return (jnp.concatenate(parts, axis=0) if len(parts) > 1 else weight).astype(BF16)
-
-
-def padded_turned(weight, offset, size):
-    width = weight.shape[0]
-    parts = []
-    if offset:
-        parts.append(jnp.zeros((width, offset), F32))
-    parts.append(jnp.transpose(weight))
-    if size - offset - width:
-        parts.append(jnp.zeros((width, size - offset - width), F32))
-    return (jnp.concatenate(parts, axis=1) if len(parts) > 1 else parts[0]).astype(BF16)
-
-
-def head_blocks(value, head_dim, offset=0, size=None):
+def head_blocks(value, head_dim):
     rows, width = value.shape
-    if size is not None and size != width:
-        parts = []
-        if offset:
-            parts.append(jnp.zeros((rows, offset), F32))
-        parts.append(value)
-        if size - offset - width:
-            parts.append(jnp.zeros((rows, size - offset - width), F32))
-        value = jnp.concatenate(parts, axis=1)
-        width = size
     blocks = [
-        jnp.where(head_mask(rows, width, head_dim, head, offset), value, 0.0).astype(BF16)
+        jnp.where(head_mask(rows, width, head_dim, head), value, 0.0).astype(BF16)
         for head in range(HEADS)
     ]
     return jnp.concatenate(blocks, axis=0)
@@ -912,14 +1031,12 @@
     return jnp.transpose(jnp.concatenate(blocks, axis=0))
 
 
-def gather_heads(value, rows, head_dim, offset=0, width=None):
+def gather_heads(value, rows, head_dim):
     total = None
     for head in range(HEADS):
         block = value[head * rows : (head + 1) * rows]
-        kept = jnp.where(head_mask(rows, value.shape[1], head_dim, head, offset), block, 0.0)
+        kept = jnp.where(head_mask(rows, value.shape[1], head_dim, head), block, 0.0)
         total = kept if total is None else total + kept
-    if width is not None and width != total.shape[1]:
-        total = total[:, offset : offset + width]
     return total
 
 
@@ -960,7 +1077,14 @@
     layer_ref,
     cells_grad_ref,
     sorted_ref,
-    peer_ref,
+    quad_ref,
+    masks_ref,
+    half_ref,
+    cotangent_half_ref,
+    layer_half_ref,
+    layer_land_ref,
+    grad_half_ref,
+    grad_land_ref,
     gathered_ref,
     keys_ref,
     keys_turned_ref,
@@ -970,16 +1094,13 @@
     banks_ref,
     blocks_ref,
     grad_blocks_ref,
-    wide_blocks_ref,
     top_ref,
     sum_ref,
     turned_ref,
     total_ref,
     value_total_ref,
-    item_w_ref,
-    item_turned_ref,
     branch_ref,
-    peer_branch_ref,
+    quad_branch_ref,
     mlp_part_ref,
     item_part_ref,
     feat_part_ref,
@@ -992,7 +1113,8 @@
     feat_land_k,
     feat_land_xy,
     feat_land_z,
-    swap_sem,
+    quad_sem,
+    side_sem,
     gather_sem,
     grads_sem,
     banks_sem,
@@ -1004,6 +1126,7 @@
     mover = Mover(move_sem)
     proj_load = mover.start(proj_in, proj_ref)
     feat_out_load = mover.start(feat_out_in, feat_out_ref)
+    cotangent_load = mover.start(cotangent_in, cotangent_ref)
     bank_loads = [
         mover.start(bank_first_in, bank_first_ref),
         mover.start(bank_second_in, bank_second_ref),
@@ -1014,33 +1137,34 @@
             (item_out_in, item_out_ref),
             (mlp_in_in, mlp_in_ref),
             (mlp_out_in, mlp_out_ref),
-            (cotangent_in, cotangent_ref),
         )
     ]
-    rows_dev, width_dev = cells_ref.shape
+    rows_dev = cells_ref.shape[0]
     width = feat_out_ref.shape[0]
-    cols_dev = width_dev // width
     head_dim = width // HEADS
     scaling = head_dim ** (-0.5)
-    ff_width = mlp_in_ref.shape[1]
-    key_total = keys_ref.shape[1]
-    chip_rows = 2 * rows_dev
+    to_log2 = scaling * math.log2(math.e)
+    key_total = keys_ref.shape[0]
+    block_rows = 2 * rows_dev
     bank_slots = bank_first_ref.shape[0]
     train_count = train_ref[0]
     me = lax.axis_index("rows")
+    quad = Quad()
     sizes = {"z": rows_count // 4, "x": 2, "k": 2, "y": cols_count}
-    own_count = cols_dev * rows_dev
 
     def shard_of(ref, rows):
         return lambda shard: ref.at[pl.ds(pl.multiple_of(shard * rows, rows), rows), :]
 
     def stats_shard(shard):
-        return all_stats_ref.at[:, pl.ds(pl.multiple_of(shard * rows_dev, rows_dev), rows_dev)]
-
-    hidden_gather = RowGather(
+        return all_stats_ref.at[:, block_span(shard)]
+
+    def block_span(shard):
+        return pl.ds(pl.multiple_of(shard * block_rows, block_rows), block_rows)
+
+    hidden_gather = DepthGather(
         [shard_of(gathered_ref, rows_dev)], gather_sem.at[0], gather_sem.at[1], rows_count
     )
-    grads_gather = RowGather(
+    grads_gather = DepthGather(
         [shard_of(grads_ref, rows_dev), stats_shard], grads_sem.at[0], grads_sem.at[1], rows_count
     )
     banks_gather = RowGather(
@@ -1070,6 +1194,9 @@
         (feat_land_k, feat_land_xy, feat_land_z),
         feat_sem,
     )
+    depth, core = hidden_gather.depth, hidden_gather.core
+    own_shard = depth * 2 + core
+    own_rows = pl.ds(pl.multiple_of(own_shard * rows_dev, rows_dev), rows_dev)
     meet(
         [
             mlp_sum.device(mlp_sum.partner(stage, j))
@@ -1078,41 +1205,68 @@
         ]
     )
 
-    swap = swap_copy(cells_ref, peer_ref, swap_sem.at[0], swap_sem.at[1])
-    swap.start()
+    cell_copies = quad.spread(cells_ref, quad_ref, quad_sem.at[0])
+    for copy in cell_copies:
+        copy.start()
+    mask_copy = quad.across(mask_ref, masks_ref.at[quad.side], side_sem.at[0])
+    mask_copy.start()
+    quad_ref[quad.own] = cells_ref[...]
+    masks_ref[quad.side] = mask_ref[...]
     for load in bank_loads:
         load.wait()
     banks_ref[pl.ds(pl.multiple_of(me * bank_slots, bank_slots), bank_slots), :] = jnp.concatenate(
         [bank_first_ref[...], bank_second_ref[...]], axis=1
     ).astype(BF16)
+    cotangent_load.wait()
+    cotangent = cotangent_ref[...].astype(F32)
+    half_ref[...] = quad.pick(cotangent, width, 1).astype(BF16)
+    cotangent_copy = quad.across(half_ref, cotangent_half_ref, side_sem.at[1])
+
+    table = head_table(width, head_dim)
+    wide = spread_table(width, head_dim)
+    proj_load.wait()
+    feat_w = [proj_ref[n].astype(BF16) for n in range(3)]
+    for copy in cell_copies:
+        copy.wait()
+    mask_copy.wait()
+    cotangent_copy.start()
     banks_gather.start_near()
     banks_gather.start_depth()
-    proj_load.wait()
-    feat_w = [proj_ref[n].astype(BF16) for n in range(3)]
-    own = stack_columns(cells_ref[...].astype(F32), width)
+    columns = quad.columns(quad_ref, width)
+    own = columns[0]
     own_low = own.astype(BF16)
-    queries, own_keys, own_values = [
-        dot_nn(own_low, weight).astype(BF16).astype(F32) for weight in feat_w
-    ]
-    table = head_table(width, head_dim)
-    wide = spread_table(width, head_dim)
-    swap.wait()
-    peer_low = stack_columns(peer_ref[...].astype(F32), width).astype(BF16)
-    peer_queries, peer_keys, peer_values = [
-        dot_nn(peer_low, weight).astype(BF16).astype(F32) for weight in feat_w
-    ]
-    feat_query = jnp.concatenate([queries, peer_queries], axis=0)
-    all_keys = jnp.concatenate([own_keys, peer_keys], axis=0)
-    all_values = jnp.concatenate([own_values, peer_values], axis=0)
-    slots = all_keys.shape[0] // rows_dev
-    own_first = lax.axis_index("cols") == 0
-    key_list = [all_keys[n * rows_dev : (n + 1) * rows_dev] for n in range(slots)]
-    value_list = [all_values[n * rows_dev : (n + 1) * rows_dev] for n in range(slots)]
-    open_list = [column_open(mask_ref, own_first, cols_dev, n) for n in range(slots)]
-    weights = feature_weights(feat_query, key_list, open_list, slots, table, scaling)
+    all_low = jnp.concatenate(columns, axis=0).astype(BF16)
+    own_query = dot_nn(own_low, feat_w[0]).astype(BF16).astype(F32)
+    feat_keys = dot_nn(all_low, feat_w[1]).astype(BF16).astype(F32)
+    feat_values = dot_nn(all_low, feat_w[2]).astype(BF16).astype(F32)
+    slots = len(columns)
+    key_list = [feat_keys[n * block_rows : (n + 1) * block_rows] for n in range(slots)]
+    value_list = [feat_values[n * block_rows : (n + 1) * block_rows] for n in range(slots)]
+    mask_blocks = []
+    for side in range(2):
+        rows = [
+            masks_ref[
+                side,
+                pl.ds(
+                    2 * (quad.col + col_flip - 2 * quad.col * col_flip)
+                    + quad.side
+                    + other
+                    - 2 * quad.side * other,
+                    1,
+                ),
+                :,
+            ]
+            for col_flip in range(2)
+            for other in range(2)
+        ]
+        rows.append(jnp.zeros((8 - slots, rows_dev), jnp.int32))
+        mask_blocks.append(jnp.transpose(jnp.concatenate(rows, axis=0).astype(F32)))
+    masks = jnp.concatenate(mask_blocks, axis=0)
+    open_list = [masks[:, n : n + 1] > 0.0 for n in range(slots)]
+    own_weights = feature_weights(own_query, key_list, open_list, 1, table, scaling)
     mixed = None
-    for weight, column_values in zip(weights, value_list):
-        added = dot_nn(weight[:own_count].astype(BF16), wide) * tile_rows(column_values, cols_dev)
+    for weight, column_values in zip(own_weights, value_list):
+        added = dot_nn(weight.astype(BF16), wide) * column_values
         mixed = added if mixed is None else mixed + added
     feat_mixed = mixed.astype(BF16)
     feat_out_load.wait()
@@ -1121,76 +1275,58 @@
     unit_one, root_one = norm_parts(first_sum)
     first_out = unit_one * gains_ref[0:1, :] + shifts_ref[0:1, :]
     first_low = first_out.astype(BF16)
-    own_rows = pl.ds(pl.multiple_of(me * rows_dev, rows_dev), rows_dev)
     gathered_ref[own_rows, :] = pack_columns(first_out, rows_dev).astype(BF16)
-    hidden_gather.start_near()
-    hidden_gather.start_depth()
+    hidden_gather.start()
 
     item_w = [proj_ref[3 + n].astype(BF16) for n in range(3)]
+    turned_w = [jnp.transpose(proj_ref[4 + n]).astype(BF16) for n in range(2)]
     queries, own_keys, own_values = [
         dot_nn(first_low, weight).astype(BF16).astype(F32) for weight in item_w
     ]
-    windows = [window_of(column, width, width_dev) for column in range(cols_dev)]
-    for column, (_, offset, size) in enumerate(windows):
-        for n in range(3):
-            item_w_ref[column, n, 0:size, :] = padded_weight(proj_ref[3 + n], offset, size)
-        for n in range(2):
-            item_turned_ref[column, n, :, 0:size] = padded_turned(proj_ref[4 + n], offset, size)
-        blocks_ref[column] = head_blocks(
-            queries[column * rows_dev : (column + 1) * rows_dev], head_dim
-        )
+    blocks_ref[...] = head_blocks(queries, head_dim)
     top_ref[...] = jnp.full(top_ref.shape, NEGATIVE, F32)
     sum_ref[...] = jnp.zeros(sum_ref.shape, F32)
     turned_ref[...] = jnp.zeros(turned_ref.shape, F32)
-    to_log2 = scaling * math.log2(math.e)
-
-    def chip_start(depth, side):
-        return pl.multiple_of((depth * 2 + side) * chip_rows, chip_rows)
-
-    def masked_scores(column, keys, start_row):
-        raw = dot_nt(keys, blocks_ref[column]) * to_log2
-        key_row = lax.broadcasted_iota(jnp.int32, raw.shape, 0)
-        return jnp.where(key_row < train_count - start_row, raw, NEGATIVE)
-
-    def attend_chip(depth, side):
-        @pl.when(depth * 4 * rows_dev < key_total)
+
+    def hidden_of(shard):
+        rows = pl.ds(pl.multiple_of(shard * rows_dev, rows_dev), rows_dev)
+        return stack_columns(gathered_ref[rows, :].astype(F32), width).astype(BF16)
+
+    def open_rows(shape, shard_depth, shard_core):
+        row = lax.broadcasted_iota(jnp.int32, shape, 0)
+        row = row + jnp.where(row >= rows_dev, rows_dev, 0)
+        return row < train_count - (shard_depth * 4 + shard_core) * rows_dev
+
+    def masked_scores(keys, shard_depth, shard_core):
+        raw = dot_nt(keys, blocks_ref[...]) * to_log2
+        return jnp.where(open_rows(raw.shape, shard_depth, shard_core), raw, NEGATIVE)
+
+    def attend(shard_depth, shard_core):
+        @pl.when(shard_depth * 2 * block_rows < key_total)
         def _():
-            start_row = chip_start(depth, side)
-            span = pl.ds(start_row, chip_rows)
-            for column, (start, _, size) in enumerate(windows):
-                hidden = gathered_ref[span, start : start + size]
-                keys = dot_nn(hidden, item_w_ref[column, 1, 0:size, :]).astype(BF16)
-                keys_ref[column, span, :] = keys
-                values_ref[column, span, :] = dot_nn(
-                    hidden, item_w_ref[column, 2, 0:size, :]
-                ).astype(BF16)
-                keys_turned_ref[column, :, span] = dot_nt(
-                    item_turned_ref[column, 0, :, 0:size], hidden
-                ).astype(BF16)
-                values_turned = dot_nt(item_turned_ref[column, 1, :, 0:size], hidden).astype(BF16)
-                scores = masked_scores(column, keys, start_row)
-                top_old = top_ref[column]
-                top_new = jnp.maximum(top_old, jnp.max(scores, axis=0, keepdims=True))
-                grown = jnp.exp2(scores - top_new)
-                fade = jnp.exp2(top_old - top_new)
-                top_ref[column] = top_new
-                sum_ref[column] = sum_ref[column] * fade + jnp.sum(grown, axis=0, keepdims=True)
-                turned_ref[column] = turned_ref[column] * fade + dot_nn(
-                    values_turned, grown.astype(BF16)
-                )
-
-    hidden_gather.run(attend_chip)
+            shard = shard_depth * 2 + shard_core
+            span = block_span(shard)
+            hidden = hidden_of(shard)
+            keys = dot_nn(hidden, item_w[1]).astype(BF16)
+            keys_ref[span, :] = keys
+            values_ref[span, :] = dot_nn(hidden, item_w[2]).astype(BF16)
+            keys_turned_ref[:, span] = dot_nt(turned_w[0], hidden).astype(BF16)
+            values_turned = dot_nt(turned_w[1], hidden).astype(BF16)
+            scores = masked_scores(keys, shard_depth, shard_core)
+            top_old = top_ref[...]
+            top_new = jnp.maximum(top_old, jnp.max(scores, axis=0, keepdims=True))
+            grown = jnp.exp2(scores - top_new)
+            fade = jnp.exp2(top_old - top_new)
+            top_ref[...] = top_new
+            sum_ref[...] = sum_ref[...] * fade + jnp.sum(grown, axis=0, keepdims=True)
+            turned_ref[...] = turned_ref[...] * fade + dot_nn(values_turned, grown.astype(BF16))
+
+    hidden_gather.run(attend, 0)
     for k in range(1, rows_count // 4):
         banks_gather.along_depth(k)
-
-    item_full, log_totals = [], []
-    for column in range(cols_dev):
-        item_full.append(
-            gather_heads_turned(turned_ref[column] / sum_ref[column], rows_dev, head_dim)
-        )
-        log_totals.append(top_ref[column] + jnp.log2(sum_ref[column]))
-
-    full = jnp.concatenate(item_full, axis=0)
+    full = gather_heads_turned(turned_ref[...] / sum_ref[...], block_rows, head_dim)
+    log_total = top_ref[...] + jnp.log2(sum_ref[...])
+
     item_low = full.astype(BF16)
     for load in later_loads:
         load.wait()
@@ -1205,9 +1341,16 @@
     hidden_low = (hidden_pre * normal).astype(BF16)
     unit_three, root_three = norm_parts(second_out + dot_nt(hidden_low, mlp_out_w))
     third_out = unit_three * gains_ref[2:3, :] + shifts_ref[2:3, :]
-    layer_ref[...] = pack_columns(third_out, rows_dev).astype(BF16)
-    results = [mover.start(layer_ref, layer_out)]
-    incoming = stack_columns(cotangent_ref[...].astype(F32), width)
+    cotangent_copy.wait()
+    own_part = quad.pick(cotangent, width, 0)
+    other_part = cotangent_half_ref[...].astype(F32)
+    incoming = jnp.concatenate(
+        [
+            jnp.where(quad.side == 0, own_part, other_part),
+            jnp.where(quad.side == 0, other_part, own_part),
+        ],
+        axis=0,
+    )
     third_grad, gain_three, shift_three = norm_back(
         unit_three, root_three, gains_ref[2:3, :], incoming
     )
@@ -1219,100 +1362,85 @@
     )
     second_grad_low = second_grad.astype(BF16)
     mixed_grad = dot_nt(second_grad_low, item_out_w).astype(BF16).astype(F32)
-    delta_all = head_rows_of(mixed_grad * full, wide)
-    deltas = []
-    spare = jnp.zeros((8 - HEADS, rows_dev), F32)
-    for column in range(cols_dev):
-        part = delta_all[0:8, column * rows_dev : (column + 1) * rows_dev]
-        deltas.append(jnp.concatenate([part[h : h + 1] for h in range(HEADS)], axis=1))
-        totals = [
-            log_totals[column][:, head * rows_dev : (head + 1) * rows_dev]
-            for head in range(HEADS)
-        ]
-        all_stats_ref[16 * column : 16 * column + 8, own_rows] = jnp.concatenate(
-            totals + [spare], axis=0
-        )
-        all_stats_ref[16 * column + 8 : 16 * column + 16, own_rows] = part
+    part = head_rows_of(mixed_grad * full, wide)[0:8, :]
+    delta = jnp.concatenate([part[h : h + 1] for h in range(HEADS)], axis=1)
+    totals = [log_total[:, h * block_rows : (h + 1) * block_rows] for h in range(HEADS)]
+    spare = jnp.zeros((8 - HEADS, block_rows), F32)
+    own_span = block_span(own_shard)
+    all_stats_ref[0:8, own_span] = jnp.concatenate(totals + [spare], axis=0)
+    all_stats_ref[8:16, own_span] = part
     grads_ref[own_rows, :] = pack_columns(mixed_grad, rows_dev).astype(BF16)
-    grads_gather.start_near()
-    grads_gather.start_depth()
+    grads_gather.start()
 
     row = put_tiles(mlp_part_ref, 0, dot_tn(second_low, pre_low))
     row = put_tiles(mlp_part_ref, row, dot_tn(branch_low, hidden_low))
     row = put_tiles(mlp_part_ref, row, dot_tn(item_low, second_grad_low))
     put_zeros(mlp_part_ref, row)
     mlp_sum.scatter_start(0)
-
-    for column in range(cols_dev):
-        rows_here = slice(column * rows_dev, (column + 1) * rows_dev)
-        grad_blocks_ref[column] = head_blocks(mixed_grad[rows_here], head_dim)
+    first_block, second_block = third_out[:rows_dev], third_out[rows_dev:]
+    layer_half_ref[...] = jnp.where(quad.side == 0, second_block, first_block).astype(BF16)
+    own_layer = jnp.where(quad.side == 0, first_block, second_block)
+
+    grad_blocks_ref[...] = head_blocks(mixed_grad, head_dim)
     turned_ref[...] = jnp.zeros(turned_ref.shape, F32)
-
-    @pl.loop(0, key_total // chip_rows)
+    key_steps = key_total // block_rows
+
+    @pl.loop(0, key_steps)
     def _(step):
-        start_row = pl.multiple_of(step * chip_rows, chip_rows)
-        span = pl.ds(start_row, chip_rows)
-        for column in range(cols_dev):
-            keys = keys_ref[column, span, :]
-            attend = jnp.exp2(masked_scores(column, keys, start_row) - log_totals[column])
-            dots = dot_nt(values_ref[column, span, :], grad_blocks_ref[column])
-            score_grad = (attend * (dots - deltas[column])).astype(BF16)
-            turned_ref[column] += dot_nn(keys_turned_ref[column, :, span], score_grad)
-
-    query_grads = [
-        gather_heads_turned(turned_ref[column], rows_dev, head_dim) * scaling
-        for column in range(cols_dev)
-    ]
+        @pl.when(step == key_steps - 2)
+        def _():
+            grads_gather.forward(1)
+
+        @pl.when(step == key_steps - 1)
+        def _():
+            grads_gather.forward(2)
+
+        span = block_span(step)
+        keys = keys_ref[span, :]
+        attend_now = jnp.exp2(masked_scores(keys, step // 2, step % 2) - log_total)
+        dots = dot_nt(values_ref[span, :], grad_blocks_ref[...])
+        score_grad = (attend_now * (dots - delta)).astype(BF16)
+        turned_ref[...] += dot_nn(keys_turned_ref[:, span], score_grad)
+
+    query_grad = gather_heads_turned(turned_ref[...], block_rows, head_dim) * scaling
+
+    blocks_ref[...] = head_blocks(own_keys, head_dim)
+    grad_blocks_ref[...] = head_blocks(own_values, head_dim)
+    total_ref[...] = jnp.zeros(total_ref.shape, F32)
+    value_total_ref[...] = jnp.zeros(value_total_ref.shape, F32)
+
+    def answer(shard_depth, shard_core):
+        shard = shard_depth * 2 + shard_core
+        span = block_span(shard)
+        asked = dot_nn(hidden_of(shard), item_w[0]).astype(BF16)
+        rows = pl.ds(pl.multiple_of(shard * rows_dev, rows_dev), rows_dev)
+        grads = stack_columns(grads_ref[rows, :].astype(F32), width).astype(BF16)
+        scores = dot_nt(blocks_ref[...], asked) * to_log2
+        dots = dot_nt(grad_blocks_ref[...], grads)
+        attends, score_grads = [], []
+        for head in range(HEADS):
+            part = slice(head * block_rows, (head + 1) * block_rows)
+            attend_now = jnp.exp2(scores[part] - all_stats_ref[head : head + 1, span])
+            attends.append(attend_now.astype(BF16))
+            score_grads.append(
+                (attend_now * (dots[part] - all_stats_ref[8 + head : 9 + head, span])).astype(BF16)
+            )
+        total_ref[...] += dot_nn(jnp.concatenate(score_grads, axis=0), asked)
+        value_total_ref[...] += dot_nn(jnp.concatenate(attends, axis=0), grads)
+
+    grads_gather.run(answer, 2)
+    layer_copy = quad.across(layer_half_ref, layer_land_ref, side_sem.at[2])
+    layer_copy.start()
     mlp_sum.scatter_finish(0)
     mlp_sum.scatter_start(1)
-    for k in range(rows_count // 4):
-        banks_gather.across_side(k)
-
-    for column, (_, offset, size) in enumerate(windows):
-        rows_here = slice(column * rows_dev, (column + 1) * rows_dev)
-        blocks_ref[column] = head_blocks(own_keys[rows_here], head_dim)
-        wide_blocks_ref[column, :, 0:size] = head_blocks(
-            own_values[rows_here], head_dim, offset, size
-        )
-    total_ref[...] = jnp.zeros(total_ref.shape, F32)
-    value_total_ref[...] = jnp.zeros(value_total_ref.shape, F32)
-
-    def answer_chip(depth, side):
-        span = pl.ds(chip_start(depth, side), chip_rows)
-        for column, (start, _, size) in enumerate(windows):
-            hidden = gathered_ref[span, start : start + size]
-            asked = dot_nn(hidden, item_w_ref[column, 0, 0:size, :]).astype(BF16)
-            grads = grads_ref[span, start : start + size]
-            scores = dot_nt(blocks_ref[column], asked) * to_log2
-            dots = dot_nt(wide_blocks_ref[column, :, 0:size], grads)
-            attends, score_grads = [], []
-            for head in range(HEADS):
-                part = slice(head * rows_dev, (head + 1) * rows_dev)
-                log_total = all_stats_ref[16 * column + head : 16 * column + head + 1, span]
-                delta = all_stats_ref[16 * column + 8 + head : 16 * column + 9 + head, span]
-                attend = jnp.exp2(scores[part] - log_total)
-                attends.append(attend.astype(BF16))
-                score_grads.append((attend * (dots[part] - delta)).astype(BF16))
-            total_ref[column] += dot_nn(jnp.concatenate(score_grads, axis=0), asked)
-            value_total_ref[column, :, 0:size] += dot_nn(jnp.concatenate(attends, axis=0), grads)
-
-    grads_gather.run(answer_chip)
-    mlp_sum.scatter_finish(1)
-    mlp_sum.scatter_start(2)
-
-    own_row = me * rows_dev + lax.broadcasted_iota(jnp.int32, (rows_dev, width), 0)
-    own_open = own_row < train_count
-    key_grads, value_grads = [], []
-    for column, (_, offset, size) in enumerate(windows):
-        key_grad = gather_heads(total_ref[column], rows_dev, head_dim) * scaling
-        value_grad = gather_heads(
-            value_total_ref[column, :, 0:size], rows_dev, head_dim, offset, width
-        )
-        key_grads.append(jnp.where(own_open, key_grad, 0.0))
-        value_grads.append(jnp.where(own_open, value_grad, 0.0))
+
+    own_open = open_rows((block_rows, width), depth, core)
+    key_grad = gather_heads(total_ref[...], block_rows, head_dim) * scaling
+    value_grad = gather_heads(value_total_ref[...], block_rows, head_dim)
     item_grads = [
-        jnp.concatenate(parts, axis=0).astype(BF16)
-        for parts in (query_grads, key_grads, value_grads)
+        query_grad.astype(BF16),
+        jnp.where(own_open, key_grad, 0.0).astype(BF16),
+        jnp.where(own_open, value_grad, 0.0).astype(BF16),
     ]
     first_grad = second_grad
     for n in range(3):
@@ -1321,8 +1449,9 @@
         unit_one, root_one, gains_ref[0:1, :], first_grad
     )
     branch_ref[...] = pack_columns(first_in_grad, rows_dev).astype(BF16)
-    swap = swap_copy(branch_ref, peer_branch_ref, swap_sem.at[2], swap_sem.at[3])
-    swap.start()
+    branch_copies = quad.spread(branch_ref, quad_branch_ref, quad_sem.at[1])
+    for copy in branch_copies:
+        copy.start()
 
     own_branch = first_in_grad.astype(BF16)
     row = put_tiles(
@@ -1346,46 +1475,68 @@
     )
     put_zeros(item_part_ref, row)
     item_sum.scatter_start(0)
-    mlp_sum.scatter_finish(2)
-    mlp_sum.gather_start(2)
+
+    other_query = dot_nn(all_low[block_rows:], feat_w[0]).astype(BF16).astype(F32)
+    others = slots - 1
+    other_weights = feature_weights(other_query, key_list, open_list, others, table, scaling)
+    own_feat_grad = dot_nt(own_branch, feat_out_w).astype(BF16).astype(F32)
+
+    def minus_mean(weights, dots):
+        row_delta = None
+        for weight, dot in zip(weights, dots):
+            added = weight * dot
+            row_delta = added if row_delta is None else row_delta + added
+        return [dot - row_delta for dot in dots]
+
+    own_dots = minus_mean(
+        own_weights, [head_sums(own_feat_grad * part, table) for part in value_list]
+    )
+    own_score_grads = [
+        (weight * dot).astype(BF16) for weight, dot in zip(own_weights, own_dots)
+    ]
+    feat_query_grad = None
+    for score_grad, part in zip(own_score_grads, key_list):
+        added = dot_nn(score_grad, wide) * part
+        feat_query_grad = added if feat_query_grad is None else feat_query_grad + added
+    mlp_sum.scatter_finish(1)
+    mlp_sum.share_start()
     item_sum.scatter_finish(0)
     item_sum.scatter_start(1)
-
-    swap.wait()
-    peer_branch = stack_columns(peer_branch_ref[...].astype(F32), width).astype(BF16)
-    all_branch = jnp.concatenate([own_branch, peer_branch], axis=0)
-    feat_grad = dot_nt(all_branch, feat_out_w).astype(BF16).astype(F32)
-    dots = [head_sums(feat_grad * tile_rows(part, slots), table) for part in value_list]
-    row_delta = None
-    for weight, dot in zip(weights, dots):
-        added = weight * dot
-        row_delta = added if row_delta is None else row_delta + added
-    score_grads = [
-        (weight * (dot - row_delta)).astype(BF16) for weight, dot in zip(weights, dots)
-    ]
-    mlp_sum.gather_finish(2)
-    mlp_sum.gather_start(1)
-    item_sum.scatter_finish(1)
-    item_sum.scatter_start(2)
-    query_grad = None
-    for score_grad, part in zip(score_grads, key_list):
-        added = dot_nn(score_grad[:own_count], wide) * tile_rows(part, cols_dev)
-        query_grad = added if query_grad is None else query_grad + added
-    key_parts, value_parts = [], []
-    for column in range(cols_dev):
-        key_products = dot_nn(score_grads[column], wide) * feat_query
-        value_products = dot_nn(weights[column].astype(BF16), wide) * feat_grad
-        key_sum = key_products[:rows_dev]
-        value_sum = value_products[:rows_dev]
-        for n in range(1, slots):
-            key_sum = key_sum + key_products[n * rows_dev : (n + 1) * rows_dev]
-            value_sum = value_sum + value_products[n * rows_dev : (n + 1) * rows_dev]
-        key_parts.append(key_sum)
-        value_parts.append(value_sum)
+    for k in range(rows_count // 4):
+        banks_gather.across_side(k)
+    for copy in branch_copies:
+        copy.wait()
+    other_branch = jnp.concatenate(
+        [
+            stack_columns(quad_branch_ref[quad.number(pattern)].astype(F32), width)
+            for pattern in range(1, 4)
+        ],
+        axis=0,
+    ).astype(BF16)
+    other_feat_grad = dot_nt(other_branch, feat_out_w).astype(BF16).astype(F32)
+    other_dots = minus_mean(
+        other_weights,
+        [head_sums(other_feat_grad * tile_rows(part, others), table) for part in value_list],
+    )
+    other_score_grad = (other_weights[0] * other_dots[0]).astype(BF16)
+
+    def own_and_others(own_part, other_part):
+        total = own_part
+        for n in range(others):
+            total = total + other_part[n * block_rows : (n + 1) * block_rows]
+        return total
+
+    feat_key_grad = own_and_others(
+        dot_nn(own_score_grads[0], wide) * own_query, dot_nn(other_score_grad, wide) * other_query
+    )
+    feat_value_grad = own_and_others(
+        dot_nn(own_weights[0].astype(BF16), wide) * own_feat_grad,
+        dot_nn(other_weights[0].astype(BF16), wide) * other_feat_grad,
+    )
     feat_grads = [
-        (query_grad * scaling).astype(BF16),
-        (jnp.concatenate(key_parts, axis=0) * scaling).astype(BF16),
-        jnp.concatenate(value_parts, axis=0).astype(BF16),
+        (feat_query_grad * scaling).astype(BF16),
+        (feat_key_grad * scaling).astype(BF16),
+        feat_value_grad.astype(BF16),
     ]
     row = put_tiles(
         feat_part_ref,
@@ -1395,16 +1546,31 @@
     row = put_tiles(feat_part_ref, row, dot_tn(own_low, feat_grads[2]))
     put_zeros(feat_part_ref, row)
     feat_sum.scatter_start(0)
-    item_sum.scatter_finish(2)
-    item_sum.gather_start(2)
+    mlp_sum.share_finish()
+    mlp_sum.gather_start(1)
+    item_sum.scatter_finish(1)
+    item_sum.share_start()
     feat_sum.scatter_finish(0)
     feat_sum.scatter_start(1)
     inner = None
     for n in range(3):
         added = dot_nt(feat_grads[n], feat_w[n])
         inner = added if inner is None else inner + added
-    cells_grad_ref[...] = pack_columns(first_in_grad + inner.astype(BF16).astype(F32), rows_dev)
-    results.append(mover.start(cells_grad_ref, cells_grad_out))
+    cells_grad = first_in_grad + inner.astype(BF16).astype(F32)
+    first_block, second_block = cells_grad[:rows_dev], cells_grad[rows_dev:]
+    grad_half_ref[...] = jnp.where(quad.side == 0, second_block, first_block)
+    own_cells_grad = jnp.where(quad.side == 0, first_block, second_block)
+    grad_copy = quad.across(grad_half_ref, grad_land_ref, side_sem.at[3])
+    layer_copy.wait()
+    layer_ref[...] = quad.joined(own_layer, layer_land_ref[...].astype(F32)).astype(BF16)
+    results = [mover.start(layer_ref, layer_out)]
+    mlp_sum.gather_finish(1)
+    mlp_sum.gather_start(0)
+    item_sum.share_finish()
+    item_sum.gather_start(1)
+    feat_sum.scatter_finish(1)
+    feat_sum.share_start()
+    grad_copy.start()
     for k in range(rows_count // 4):
         banks_gather.from_core(k, 0)
         banks_gather.from_core(k, 1)
@@ -1421,26 +1587,21 @@
             sorted_ref[pl.ds(start, sort_block), :] = dot_nn(chosen, banks_ref[...]).astype(BF16)
 
     thirds = sort_rows // sort_block // 3
-    mlp_sum.gather_finish(1)
-    mlp_sum.gather_start(0)
-    item_sum.gather_finish(2)
-    item_sum.gather_start(1)
-    feat_sum.scatter_finish(1)
-    feat_sum.scatter_start(2)
     sort_some(0, thirds)
+    mlp_sum.gather_finish(0)
     item_sum.gather_finish(1)
     item_sum.gather_start(0)
-    feat_sum.scatter_finish(2)
-    feat_sum.gather_start(2)
+    feat_sum.share_finish()
+    feat_sum.gather_start(1)
     sort_some(thirds, 2 * thirds)
-    feat_sum.gather_finish(2)
-    feat_sum.gather_start(1)
+    feat_sum.gather_finish(1)
+    feat_sum.gather_start(0)
+    grad_copy.wait()
+    cells_grad_ref[...] = quad.joined(own_cells_grad, grad_land_ref[...])
+    results.append(mover.start(cells_grad_ref, cells_grad_out))
     sort_some(2 * thirds, sort_rows // sort_block)
     results.append(mover.start(sorted_ref, sorted_out))
-    mlp_sum.gather_finish(0)
     item_sum.gather_finish(0)
-    feat_sum.gather_finish(1)
-    feat_sum.gather_start(0)
     for gather in (hidden_gather, grads_gather, banks_gather):
         gather.wait_sent()
     for result in results:
@@ -1687,14 +1848,11 @@
     rows_dev, width_dev = cells.shape
     width = proj_weights.shape[-1]
     ff_width = mlp_in.shape[1]
-    cols_dev = width_dev // width
     rows_all = rows_dev * rows_count
     key_total = rows_all // 4 * 3
-    head_rows = HEADS * rows_dev
-    slots = RowGather.slots(rows_count)
+    head_rows = HEADS * 2 * rows_dev
     dma = pltpu.SemaphoreType.DMA
     shape = jax.ShapeDtypeStruct
-    devices = rows_count * cols_count
     sizes = {"z": rows_count // 4, "x": 2, "k": 2, "y": cols_count}
 
     mask_rows = feat_mask.T
@@ -1704,15 +1862,16 @@
     bank_rows = owner_rows.shape[0]
 
     def block_rows(rows):
-        return -(-rows // (16 * devices)) * 16 * devices
+        unit = 16 * math.prod(members(stage, sizes) for stage in STAGES[:-1])
+        return -(-rows // unit) * unit
 
     def landings(rows):
         found = []
-        for stage in STAGES:
+        for stage in STAGES[:-1]:
             count = members(stage, sizes)
             rows //= count
             found.append(pltpu.VMEM((count - 1, rows, LANES), BF16))
-        return found
+        return found + [pltpu.VMEM((members(STAGES[-1], sizes), rows, LANES), BF16)]
 
     both_tiles = 2 * width // LANES * width
     half_tiles = -(-width // LANES) * width
@@ -1745,34 +1904,39 @@
             pltpu.VMEM((rows_dev, width_dev), BF16),
             pltpu.VMEM((rows_dev, width_dev), F32),
             pltpu.VMEM((bank_rows, 2 * width), BF16),
+            pltpu.VMEM((4, rows_dev, width_dev), BF16),
+            pltpu.VMEM((2,) + mask_rows.shape, jnp.int32),
+            pltpu.VMEM((rows_dev, width), BF16),
+            pltpu.VMEM((rows_dev, width), BF16),
+            pltpu.VMEM((rows_dev, width), BF16),
+            pltpu.VMEM((rows_dev, width), BF16),
+            pltpu.VMEM((rows_dev, width), F32),
+            pltpu.VMEM((rows_dev, width), F32),
+            pltpu.VMEM((rows_all // 2, width_dev), BF16),
+            pltpu.VMEM((key_total, width), BF16),
+            pltpu.VMEM((width, key_total), BF16),
+            pltpu.VMEM((key_total, width), BF16),
+            pltpu.VMEM((rows_all // 2, width_dev), BF16),
+            pltpu.VMEM((16, rows_all), F32),
+            pltpu.VMEM((bank_rows, 2 * width), BF16),
+            pltpu.VMEM((head_rows, width), BF16),
+            pltpu.VMEM((head_rows, width), BF16),
+            pltpu.VMEM((1, head_rows), F32),
+            pltpu.VMEM((1, head_rows), F32),
+            pltpu.VMEM((width, head_rows), F32),
+            pltpu.VMEM((head_rows, width), F32),
+            pltpu.VMEM((head_rows, width), F32),
             pltpu.VMEM((rows_dev, width_dev), BF16),
-            pltpu.VMEM((rows_all, width_dev), BF16),
-            pltpu.VMEM((cols_dev, key_total, width), BF16),
-            pltpu.VMEM((cols_dev, width, key_total), BF16),
-            pltpu.VMEM((cols_dev, key_total, width), BF16),
-            pltpu.VMEM((rows_all, width_dev), BF16),
-            pltpu.VMEM((16 * cols_dev, rows_all), F32),
-            pltpu.VMEM((bank_rows, 2 * width), BF16),
-            pltpu.VMEM((cols_dev, head_rows, width), BF16),
-            pltpu.VMEM((cols_dev, head_rows, width), BF16),
-            pltpu.VMEM((cols_dev, head_rows, 2 * LANES), BF16),
-            pltpu.VMEM((cols_dev, 1, head_rows), F32),
-            pltpu.VMEM((cols_dev, 1, head_rows), F32),
-            pltpu.VMEM((cols_dev, width, head_rows), F32),
-            pltpu.VMEM((cols_dev, head_rows, width), F32),
-            pltpu.VMEM((cols_dev, head_rows, 2 * LANES), F32),
-            pltpu.VMEM((cols_dev, 3, 2 * LANES, width), BF16),
-            pltpu.VMEM((cols_dev, 2, width, 2 * LANES), BF16),
-            pltpu.VMEM((rows_dev, width_dev), BF16),
-            pltpu.VMEM((rows_dev, width_dev), BF16),
+            pltpu.VMEM((4, rows_dev, width_dev), BF16),
         ]
         + [pltpu.VMEM((rows, LANES), BF16) for rows in sum_rows]
         + [landing for rows in sum_rows for landing in landings(rows)]
         + [
-            dma((4,)),
-            dma((2, 1, slots)),
-            dma((2, 2, slots)),
-            dma((2, 1, slots)),
+            dma((2, 2, 3)),
+            dma((4, 2)),
+            dma((2, 1, DepthGather.slots(rows_count))),
+            dma((2, 2, DepthGather.slots(rows_count))),
+            dma((2, 1, RowGather.slots(rows_count))),
         ]
         + [dma((4, len(STAGES), widest))] * len(sum_rows)
         + [dma((11,))],

time: 114 us -> 102 us (0.89)
  Pallas kernels: 112 us -> 100 us
    pallas_call x1, Pallas kernels: 99.3 us -> 87.4 us  [fast_device(): pl.pallas_call(functools.partial(layer_kernel, rows_count, cols_count), n...]
where the time goes in v2:
time: 102 us
  Pallas kernels  100 us (98%)
  between operations  1.47 us (1%)
    pallas_call x1, Pallas kernels, fast_device(): pl.pallas_call(functools.partial(layer_kernel, rows_count, cols_count), n...  87.4 us
    pallas_call x1, Pallas kernels, fast_device(): pl.pallas_call(update_kernel, name='rotated_update', out_shape=(shape(lay...  12.7 us

profile of v2, /device:TPU:0, one launch (start us, length us, event | category | flops | bytes accessed | tf_op | source)
XLA Modules:
  0.0 101.6 jit_solution(16377505330351066573)
XLA Ops:
  1.3 87.4 %layer_and_gradients.1 = (bf16[128,384]{1,0:T(8,128)(2,1)}, f32[128,384]{1,0:T(8,128)}, bf16[1536,128]{1,0:T(8,128)(2,1)}, bf16[1280,128]{1,0:T(8,128)(2,1)}, bf...) custom-call(s32[1]{0:T(128)S(6)} %copy.36.train_ref, s32[2304]{0:T(1024)} %owner_ref.3, bf16[128,384]{1,0:T(8,128)(2,1)} %cells_ref.1, ...), custom_call_target="tpu_custom_call" | custom-call | tf_op jit(solution)/shard_map/layer_and_gradients/pallas_call | solution.py:1884
  88.7 12.7 %rotated_update.1 = (bf16[128,384]{1,0:T(8,128)(2,1)}, f32[128,384]{1,0:T(8,128)}, f32[8,192,192]{2,1,0:T(8,128)}, f32[192,384]{1,0:T(8,128)}, f32[192,384]{1,0:...) custom-call(s32[2304]{0:T(1024)} %owner_ref.3, ...), custom_call_target="tpu_custom_call" | custom-call | tf_op jit(solution)/shard_map/rotated_update/pallas_call | solution.py:1984

commit v3 on v2

--- a/solution.py
+++ b/solution.py
@@ -563,6 +563,10 @@
     return dot_nn(high, table) + dot_nn(low, table)
 
 
+def head_sums_low(value, table):
+    return dot_nn(value.astype(BF16), table)
+
+
 def head_mask(rows, width, head_dim, head):
     feature = lax.broadcasted_iota(jnp.int32, (rows, width), 1)
     return (feature >= head * head_dim) & (feature < (head + 1) * head_dim)
@@ -572,11 +576,12 @@
     return jnp.concatenate([value] * count, axis=0)
 
 
-def feature_weights(queries, key_list, open_list, repeat, table, scaling):
-    scores = []
-    for keys, is_open in zip(key_list, open_list):
-        raw = head_sums(queries * tile_rows(keys, repeat), table) * scaling
-        scores.append(jnp.where(tile_rows(is_open, repeat), raw, NEGATIVE))
+def feature_scores(queries, keys, is_open, repeat, table, scaling):
+    raw = head_sums(queries * tile_rows(keys, repeat), table) * scaling
+    return jnp.where(tile_rows(is_open, repeat), raw, NEGATIVE)
+
+
+def softmax_of(scores):
     top = scores[0]
     for extra in scores[1:]:
         top = jnp.maximum(top, extra)
@@ -584,7 +589,8 @@
     total = grown[0]
     for extra in grown[1:]:
         total = total + extra
-    return [part / total for part in grown]
+    inverse = 1.0 / total
+    return [part * inverse for part in grown]
 
 
 def flip(value, pattern, size):
@@ -824,16 +830,13 @@
             [jnp.where(self.side == 0, own, other), jnp.where(self.side == 0, other, own)], axis=1
         )
 
-    def columns(self, landing, width):
-        found = []
-        for col_flip in range(2):
-            col = self.col + col_flip - 2 * self.col * col_flip
-            blocks = [landing[side * 2 + col].astype(F32) for side in range(2)]
-            for other in range(2):
-                found.append(
-                    jnp.concatenate([self.pick(block, width, other) for block in blocks], axis=0)
-                )
-        return found
+    def columns(self, landing, width, col_flip):
+        col = self.col + col_flip - 2 * self.col * col_flip
+        blocks = [landing[side * 2 + col].astype(F32) for side in range(2)]
+        return [
+            jnp.concatenate([self.pick(block, width, other) for block in blocks], axis=0)
+            for other in range(2)
+        ]
 
 
 class StagedSum:
@@ -1086,7 +1089,6 @@
     grad_half_ref,
     grad_land_ref,
     gathered_ref,
-    keys_ref,
     keys_turned_ref,
     values_ref,
     grads_ref,
@@ -1094,6 +1096,7 @@
     banks_ref,
     blocks_ref,
     grad_blocks_ref,
+    scores_ref,
     top_ref,
     sum_ref,
     turned_ref,
@@ -1144,7 +1147,7 @@
     head_dim = width // HEADS
     scaling = head_dim ** (-0.5)
     to_log2 = scaling * math.log2(math.e)
-    key_total = keys_ref.shape[0]
+    key_total = values_ref.shape[0]
     block_rows = 2 * rows_dev
     bank_slots = bank_first_ref.shape[0]
     train_count = train_ref[0]
@@ -1217,6 +1220,7 @@
     banks_ref[pl.ds(pl.multiple_of(me * bank_slots, bank_slots), bank_slots), :] = jnp.concatenate(
         [bank_first_ref[...], bank_second_ref[...]], axis=1
     ).astype(BF16)
+    banks_gather.start_depth()
     cotangent_load.wait()
     cotangent = cotangent_ref[...].astype(F32)
     half_ref[...] = quad.pick(cotangent, width, 1).astype(BF16)
@@ -1226,23 +1230,10 @@
     wide = spread_table(width, head_dim)
     proj_load.wait()
     feat_w = [proj_ref[n].astype(BF16) for n in range(3)]
-    for copy in cell_copies:
-        copy.wait()
+    slots = 4
+    mask_blocks = []
+    cell_copies[0].wait()
     mask_copy.wait()
-    cotangent_copy.start()
-    banks_gather.start_near()
-    banks_gather.start_depth()
-    columns = quad.columns(quad_ref, width)
-    own = columns[0]
-    own_low = own.astype(BF16)
-    all_low = jnp.concatenate(columns, axis=0).astype(BF16)
-    own_query = dot_nn(own_low, feat_w[0]).astype(BF16).astype(F32)
-    feat_keys = dot_nn(all_low, feat_w[1]).astype(BF16).astype(F32)
-    feat_values = dot_nn(all_low, feat_w[2]).astype(BF16).astype(F32)
-    slots = len(columns)
-    key_list = [feat_keys[n * block_rows : (n + 1) * block_rows] for n in range(slots)]
-    value_list = [feat_values[n * block_rows : (n + 1) * block_rows] for n in range(slots)]
-    mask_blocks = []
     for side in range(2):
         rows = [
             masks_ref[
@@ -1263,7 +1254,30 @@
         mask_blocks.append(jnp.transpose(jnp.concatenate(rows, axis=0).astype(F32)))
     masks = jnp.concatenate(mask_blocks, axis=0)
     open_list = [masks[:, n : n + 1] > 0.0 for n in range(slots)]
-    own_weights = feature_weights(own_query, key_list, open_list, 1, table, scaling)
+    columns, key_list, value_list, scores = [], [], [], []
+    for col_flip in range(2):
+        if col_flip == 1:
+            cell_copies[1].wait()
+            cell_copies[2].wait()
+        columns += quad.columns(quad_ref, width, col_flip)
+        if col_flip == 0:
+            own = columns[0]
+            own_low = own.astype(BF16)
+            own_query = dot_nn(own_low, feat_w[0]).astype(BF16).astype(F32)
+        pair = jnp.concatenate(columns[-2:], axis=0).astype(BF16)
+        pair_keys = dot_nn(pair, feat_w[1]).astype(BF16).astype(F32)
+        pair_values = dot_nn(pair, feat_w[2]).astype(BF16).astype(F32)
+        for n in range(2):
+            rows = slice(n * block_rows, (n + 1) * block_rows)
+            key_list.append(pair_keys[rows])
+            value_list.append(pair_values[rows])
+            scores.append(
+                feature_scores(own_query, pair_keys[rows], open_list[len(scores)], 1, table, scaling)
+            )
+    cotangent_copy.start()
+    banks_gather.start_near()
+    all_low = jnp.concatenate(columns, axis=0).astype(BF16)
+    own_weights = softmax_of(scores)
     mixed = None
     for weight, column_values in zip(own_weights, value_list):
         added = dot_nn(weight.astype(BF16), wide) * column_values
@@ -1308,11 +1322,11 @@
             span = block_span(shard)
             hidden = hidden_of(shard)
             keys = dot_nn(hidden, item_w[1]).astype(BF16)
-            keys_ref[span, :] = keys
             values_ref[span, :] = dot_nn(hidden, item_w[2]).astype(BF16)
             keys_turned_ref[:, span] = dot_nt(turned_w[0], hidden).astype(BF16)
             values_turned = dot_nt(turned_w[1], hidden).astype(BF16)
             scores = masked_scores(keys, shard_depth, shard_core)
+            scores_ref[span, :] = scores
             top_old = top_ref[...]
             top_new = jnp.maximum(top_old, jnp.max(scores, axis=0, keepdims=True))
             grown = jnp.exp2(scores - top_new)
@@ -1387,21 +1401,14 @@
 
     @pl.loop(0, key_steps)
     def _(step):
-        @pl.when(step == key_steps - 2)
-        def _():
-            grads_gather.forward(1)
-
-        @pl.when(step == key_steps - 1)
-        def _():
-            grads_gather.forward(2)
-
         span = block_span(step)
-        keys = keys_ref[span, :]
-        attend_now = jnp.exp2(masked_scores(keys, step // 2, step % 2) - log_total)
+        attend_now = jnp.exp2(scores_ref[span, :] - log_total)
         dots = dot_nt(values_ref[span, :], grad_blocks_ref[...])
         score_grad = (attend_now * (dots - delta)).astype(BF16)
         turned_ref[...] += dot_nn(keys_turned_ref[:, span], score_grad)
 
+    mlp_sum.scatter_finish(0)
+    mlp_sum.scatter_start(1)
     query_grad = gather_heads_turned(turned_ref[...], block_rows, head_dim) * scaling
 
     blocks_ref[...] = head_blocks(own_keys, head_dim)
@@ -1428,11 +1435,11 @@
         total_ref[...] += dot_nn(jnp.concatenate(score_grads, axis=0), asked)
         value_total_ref[...] += dot_nn(jnp.concatenate(attends, axis=0), grads)
 
-    grads_gather.run(answer, 2)
+    grads_gather.run(answer, 0)
     layer_copy = quad.across(layer_half_ref, layer_land_ref, side_sem.at[2])
     layer_copy.start()
-    mlp_sum.scatter_finish(0)
-    mlp_sum.scatter_start(1)
+    mlp_sum.scatter_finish(1)
+    mlp_sum.share_start()
 
     own_open = open_rows((block_rows, width), depth, core)
     key_grad = gather_heads(total_ref[...], block_rows, head_dim) * scaling
@@ -1478,7 +1485,12 @@
 
     other_query = dot_nn(all_low[block_rows:], feat_w[0]).astype(BF16).astype(F32)
     others = slots - 1
-    other_weights = feature_weights(other_query, key_list, open_list, others, table, scaling)
+    other_weights = softmax_of(
+        [
+            feature_scores(other_query, keys, is_open, others, table, scaling)
+            for keys, is_open in zip(key_list, open_list)
+        ]
+    )
     own_feat_grad = dot_nt(own_branch, feat_out_w).astype(BF16).astype(F32)
 
     def minus_mean(weights, dots):
@@ -1498,41 +1510,22 @@
     for score_grad, part in zip(own_score_grads, key_list):
         added = dot_nn(score_grad, wide) * part
         feat_query_grad = added if feat_query_grad is None else feat_query_grad + added
-    mlp_sum.scatter_finish(1)
-    mlp_sum.share_start()
     item_sum.scatter_finish(0)
     item_sum.scatter_start(1)
-    for k in range(rows_count // 4):
-        banks_gather.across_side(k)
-    for copy in branch_copies:
-        copy.wait()
-    other_branch = jnp.concatenate(
-        [
-            stack_columns(quad_branch_ref[quad.number(pattern)].astype(F32), width)
-            for pattern in range(1, 4)
-        ],
-        axis=0,
-    ).astype(BF16)
-    other_feat_grad = dot_nt(other_branch, feat_out_w).astype(BF16).astype(F32)
-    other_dots = minus_mean(
-        other_weights,
-        [head_sums(other_feat_grad * tile_rows(part, others), table) for part in value_list],
-    )
-    other_score_grad = (other_weights[0] * other_dots[0]).astype(BF16)
-
-    def own_and_others(own_part, other_part):
-        total = own_part
-        for n in range(others):
-            total = total + other_part[n * block_rows : (n + 1) * block_rows]
-        return total
-
-    feat_key_grad = own_and_others(
-        dot_nn(own_score_grads[0], wide) * own_query, dot_nn(other_score_grad, wide) * other_query
-    )
-    feat_value_grad = own_and_others(
-        dot_nn(own_weights[0].astype(BF16), wide) * own_feat_grad,
-        dot_nn(other_weights[0].astype(BF16), wide) * other_feat_grad,
-    )
+    mlp_sum.share_finish()
+    mlp_sum.gather_start(1)
+    feat_key_grad = dot_nn(own_score_grads[0], wide) * own_query
+    feat_value_grad = dot_nn(own_weights[0].astype(BF16), wide) * own_feat_grad
+    for n, pattern in enumerate((1, 2, 3)):
+        branch_copies[pattern - 1].wait()
+        rows = slice(n * block_rows, (n + 1) * block_rows)
+        branch = stack_columns(quad_branch_ref[quad.number(pattern)].astype(F32), width)
+        grad = dot_nt(branch.astype(BF16), feat_out_w).astype(BF16).astype(F32)
+        part_weights = [weight[rows] for weight in other_weights]
+        part_dots = minus_mean(part_weights, [head_sums(grad * part, table) for part in value_list])
+        score_grad = (part_weights[0] * part_dots[0]).astype(BF16)
+        feat_key_grad = feat_key_grad + dot_nn(score_grad, wide) * other_query[rows]
+        feat_value_grad = feat_value_grad + dot_nn(part_weights[0].astype(BF16), wide) * grad
     feat_grads = [
         (feat_query_grad * scaling).astype(BF16),
         (feat_key_grad * scaling).astype(BF16),
@@ -1546,12 +1539,14 @@
     row = put_tiles(feat_part_ref, row, dot_tn(own_low, feat_grads[2]))
     put_zeros(feat_part_ref, row)
     feat_sum.scatter_start(0)
-    mlp_sum.share_finish()
-    mlp_sum.gather_start(1)
     item_sum.scatter_finish(1)
     item_sum.share_start()
     feat_sum.scatter_finish(0)
     feat_sum.scatter_start(1)
+    mlp_sum.gather_finish(1)
+    mlp_sum.gather_start(0)
+    for k in range(rows_count // 4):
+        banks_gather.across_side(k)
     inner = None
     for n in range(3):
         added = dot_nt(feat_grads[n], feat_w[n])
@@ -1564,12 +1559,10 @@
     layer_copy.wait()
     layer_ref[...] = quad.joined(own_layer, layer_land_ref[...].astype(F32)).astype(BF16)
     results = [mover.start(layer_ref, layer_out)]
-    mlp_sum.gather_finish(1)
-    mlp_sum.gather_start(0)
+    feat_sum.scatter_finish(1)
+    feat_sum.share_start()
     item_sum.share_finish()
     item_sum.gather_start(1)
-    feat_sum.scatter_finish(1)
-    feat_sum.share_start()
     grad_copy.start()
     for k in range(rows_count // 4):
         banks_gather.from_core(k, 0)
@@ -1588,11 +1581,10 @@
 
     thirds = sort_rows // sort_block // 3
     sort_some(0, thirds)
-    mlp_sum.gather_finish(0)
+    feat_sum.share_finish()
+    feat_sum.gather_start(1)
     item_sum.gather_finish(1)
     item_sum.gather_start(0)
-    feat_sum.share_finish()
-    feat_sum.gather_start(1)
     sort_some(thirds, 2 * thirds)
     feat_sum.gather_finish(1)
     feat_sum.gather_start(0)
@@ -1601,6 +1593,7 @@
     results.append(mover.start(cells_grad_ref, cells_grad_out))
     sort_some(2 * thirds, sort_rows // sort_block)
     results.append(mover.start(sorted_ref, sorted_out))
+    mlp_sum.gather_finish(0)
     item_sum.gather_finish(0)
     for gather in (hidden_gather, grads_gather, banks_gather):
         gather.wait_sent()
@@ -1634,6 +1627,8 @@
     norm_second_ref,
     first_ref,
     second_ref,
+    layer_in,
+    cells_grad_in,
     small_in,
     big_in,
     sorted_in,
@@ -1642,8 +1637,6 @@
     item_out_in,
     mlp_in_in,
     mlp_out_in,
-    layer_in,
-    cells_grad_in,
     layer_out,
     cells_grad_out,
     square_grad_out,
@@ -1913,7 +1906,6 @@
             pltpu.VMEM((rows_dev, width), F32),
             pltpu.VMEM((rows_dev, width), F32),
             pltpu.VMEM((rows_all // 2, width_dev), BF16),
-            pltpu.VMEM((key_total, width), BF16),
             pltpu.VMEM((width, key_total), BF16),
             pltpu.VMEM((key_total, width), BF16),
             pltpu.VMEM((rows_all // 2, width_dev), BF16),
@@ -1921,6 +1913,7 @@
             pltpu.VMEM((bank_rows, 2 * width), BF16),
             pltpu.VMEM((head_rows, width), BF16),
             pltpu.VMEM((head_rows, width), BF16),
+            pltpu.VMEM((key_total, head_rows), F32),
             pltpu.VMEM((1, head_rows), F32),
             pltpu.VMEM((1, head_rows), F32),
             pltpu.VMEM((width, head_rows), F32),
@@ -2004,7 +1997,7 @@
             shape(norm_first_turned.shape, F32),
             shape(norm_first_turned.shape, F32),
         ),
-        in_specs=[in_smem()] + [in_vmem()] * 9 + [anywhere()] * 10,
+        in_specs=[in_smem()] + [in_vmem()] * 11 + [anywhere()] * 8,
         out_specs=[anywhere()] * 5
         + [in_vmem(), in_smem(), in_vmem(), in_vmem()]
         + [anywhere()] * 6
@@ -2041,6 +2034,8 @@
         norm_second_turned,
         bank_first,
         bank_second,
+        layer_part,
+        cells_part,
         bases_small,
         bases_big,
         sorted_banks,
@@ -2049,8 +2044,6 @@
         item_out_w,
         mlp_in,
         mlp_out_turned,
-        layer_part,
-        cells_part,
     )
     return (
         layer_out,

time: 102 us -> 89.4 us (0.88)
  Pallas kernels: 100 us -> 87.8 us
    pallas_call x1, Pallas kernels: 87.4 us -> 76.1 us  [fast_device(): pl.pallas_call(functools.partial(layer_kernel, rows_count, cols_count), n...]
    pallas_call x1, Pallas kernels: 12.7 us -> 11.6 us  [fast_device(): pl.pallas_call(update_kernel, name='rotated_update', out_shape=(shape(lay...]
where the time goes in v3:
time: 89.4 us; the launch traced here: 89.2 us
  Pallas kernels  87.8 us (98%)
  between operations  1.47 us (2%)
    pallas_call x1, Pallas kernels, fast_device(): pl.pallas_call(functools.partial(layer_kernel, rows_count, cols_count), n...  76.1 us
    pallas_call x1, Pallas kernels, fast_device(): pl.pallas_call(update_kernel, name='rotated_update', out_shape=(shape(lay...  11.6 us

profile of v3, /device:TPU:0, one launch (start us, length us, event | category | flops | bytes accessed | tf_op | source)
XLA Modules:
  0.0 89.2 jit_solution(5673885849211655420)
XLA Ops:
  1.3 76.1 %layer_and_gradients.1 = (bf16[128,384]{1,0:T(8,128)(2,1)}, f32[128,384]{1,0:T(8,128)}, bf16[1536,128]{1,0:T(8,128)(2,1)}, bf16[1280,128]{1,0:T(8,128)(2,1)}, bf...) custom-call(s32[1]{0:T(128)S(6)} %copy.36.train_ref, s32[2304]{0:T(1024)} %owner_ref.3, bf16[128,384]{1,0:T(8,128)(2,1)} %cells_ref.1, ...), custom_call_target="tpu_custom_call" | custom-call | tf_op jit(solution)/shard_map/layer_and_gradients/pallas_call | solution.py:1877
  77.4 11.6 %rotated_update.1 = (bf16[128,384]{1,0:T(8,128)(2,1)}, f32[128,384]{1,0:T(8,128)}, f32[8,192,192]{2,1,0:T(8,128)}, f32[192,384]{1,0:T(8,128)}, f32[192,384]{1,0:...) custom-call(s32[2304]{0:T(1024)} %owner_ref.3, ...), custom_call_target="tpu_custom_call" | custom-call | tf_op jit(solution)/shard_map/rotated_update/pallas_call | solution.py:1977

commit v4 on v3

--- a/solution.py
+++ b/solution.py
@@ -1399,7 +1399,7 @@
     turned_ref[...] = jnp.zeros(turned_ref.shape, F32)
     key_steps = key_total // block_rows
 
-    @pl.loop(0, key_steps)
+    @pl.loop(0, key_steps, unroll=2)
     def _(step):
         span = block_span(step)
         attend_now = jnp.exp2(scores_ref[span, :] - log_total)
@@ -1579,19 +1579,20 @@
             chosen = jnp.where(owner == row, 1.0, 0.0).astype(BF16)
             sorted_ref[pl.ds(start, sort_block), :] = dot_nn(chosen, banks_ref[...]).astype(BF16)
 
-    thirds = sort_rows // sort_block // 3
-    sort_some(0, thirds)
+    sort_steps = sort_rows // sort_block
+    most, nearly = 5 * sort_steps // 9, 8 * sort_steps // 9
+    sort_some(0, most)
     feat_sum.share_finish()
     feat_sum.gather_start(1)
     item_sum.gather_finish(1)
     item_sum.gather_start(0)
-    sort_some(thirds, 2 * thirds)
+    sort_some(most, nearly)
     feat_sum.gather_finish(1)
     feat_sum.gather_start(0)
     grad_copy.wait()
     cells_grad_ref[...] = quad.joined(own_cells_grad, grad_land_ref[...])
     results.append(mover.start(cells_grad_ref, cells_grad_out))
-    sort_some(2 * thirds, sort_rows // sort_block)
+    sort_some(nearly, sort_steps)
     results.append(mover.start(sorted_ref, sorted_out))
     mlp_sum.gather_finish(0)
     item_sum.gather_finish(0)

time: 89.4 us -> 87 us (0.973)
  Pallas kernels: 87.8 us -> 85.4 us
    pallas_call x1, Pallas kernels: 76.1 us -> 73.7 us  [fast_device(): pl.pallas_call(functools.partial(layer_kernel, rows_count, cols_count), n...]
where the time goes in v4:
time: 87 us; the launch traced here: 86.8 us
  Pallas kernels  85.4 us (98%)
  between operations  1.47 us (2%)
    pallas_call x1, Pallas kernels, fast_device(): pl.pallas_call(functools.partial(layer_kernel, rows_count, cols_count), n...  73.7 us
    pallas_call x1, Pallas kernels, fast_device(): pl.pallas_call(update_kernel, name='rotated_update', out_shape=(shape(lay...  11.6 us

profile of v4, /device:TPU:0, one launch (start us, length us, event | category | flops | bytes accessed | tf_op | source)
XLA Modules:
  0.0 86.8 jit_solution(739293772409628191)
XLA Ops:
  1.3 73.7 %layer_and_gradients.1 = (bf16[128,384]{1,0:T(8,128)(2,1)}, f32[128,384]{1,0:T(8,128)}, bf16[1536,128]{1,0:T(8,128)(2,1)}, bf16[1280,128]{1,0:T(8,128)(2,1)}, bf...) custom-call(s32[1]{0:T(128)S(6)} %copy.36.train_ref, s32[2304]{0:T(1024)} %owner_ref.3, bf16[128,384]{1,0:T(8,128)(2,1)} %cells_ref.1, ...), custom_call_target="tpu_custom_call" | custom-call | tf_op jit(solution)/shard_map/layer_and_gradients/pallas_call | solution.py:1878
  75.0 11.6 %rotated_update.1 = (bf16[128,384]{1,0:T(8,128)(2,1)}, f32[128,384]{1,0:T(8,128)}, f32[8,192,192]{2,1,0:T(8,128)}, f32[192,384]{1,0:T(8,128)}, f32[192,384]{1,0:...) custom-call(s32[2304]{0:T(1024)} %owner_ref.3, ...), custom_call_target="tpu_custom_call" | custom-call | tf_op jit(solution)/shard_map/rotated_update/pallas_call | solution.py:1978

commit v5 on v4

--- a/solution.py
+++ b/solution.py
@@ -1501,7 +1501,7 @@
         return [dot - row_delta for dot in dots]
 
     own_dots = minus_mean(
-        own_weights, [head_sums(own_feat_grad * part, table) for part in value_list]
+        own_weights, [head_sums_low(own_feat_grad * part, table) for part in value_list]
     )
     own_score_grads = [
         (weight * dot).astype(BF16) for weight, dot in zip(own_weights, own_dots)
@@ -1522,7 +1522,7 @@
         branch = stack_columns(quad_branch_ref[quad.number(pattern)].astype(F32), width)
         grad = dot_nt(branch.astype(BF16), feat_out_w).astype(BF16).astype(F32)
         part_weights = [weight[rows] for weight in other_weights]
-        part_dots = minus_mean(part_weights, [head_sums(grad * part, table) for part in value_list])
+        part_dots = minus_mean(part_weights, [head_sums_low(grad * part, table) for part in value_list])
         score_grad = (part_weights[0] * part_dots[0]).astype(BF16)
         feat_key_grad = feat_key_grad + dot_nn(score_grad, wide) * other_query[rows]
         feat_value_grad = feat_value_grad + dot_nn(part_weights[0].astype(BF16), wide) * grad

time: 87 us -> 86.8 us (level)
  no operation moved by 1% of the time
where the time goes in v5:
time: 86.8 us; the launch traced here: 86.6 us
  Pallas kernels  85.2 us (98%)
  between operations  1.47 us (2%)
    pallas_call x1, Pallas kernels, fast_device(): pl.pallas_call(functools.partial(layer_kernel, rows_count, cols_count), n...  73.5 us
    pallas_call x1, Pallas kernels, fast_device(): pl.pallas_call(update_kernel, name='rotated_update', out_shape=(shape(lay...  11.6 us

profile of v5, /device:TPU:0, one launch (start us, length us, event | category | flops | bytes accessed | tf_op | source)
XLA Modules:
  0.0 86.6 jit_solution(15375561605504133055)
XLA Ops:
  1.3 73.5 %layer_and_gradients.1 = (bf16[128,384]{1,0:T(8,128)(2,1)}, f32[128,384]{1,0:T(8,128)}, bf16[1536,128]{1,0:T(8,128)(2,1)}, bf16[1280,128]{1,0:T(8,128)(2,1)}, bf...) custom-call(s32[1]{0:T(128)S(6)} %copy.36.train_ref, s32[2304]{0:T(1024)} %owner_ref.3, bf16[128,384]{1,0:T(8,128)(2,1)} %cells_ref.1, ...), custom_call_target="tpu_custom_call" | custom-call | tf_op jit(solution)/shard_map/layer_and_gradients/pallas_call | solution.py:1878
  74.8 11.6 %rotated_update.1 = (bf16[128,384]{1,0:T(8,128)(2,1)}, f32[128,384]{1,0:T(8,128)}, f32[8,192,192]{2,1,0:T(8,128)}, f32[192,384]{1,0:T(8,128)}, f32[192,384]{1,0:...) custom-call(s32[2304]{0:T(1024)} %owner_ref.3, ...), custom_call_target="tpu_custom_call" | custom-call | tf_op jit(solution)/shard_map/rotated_update/pallas_call | solution.py:1978
